TPU v7x, 32 devices: a whole 2x2x4 slice. The times are simulated.
32 devices in a mesh: dp: 16 (over z, x, core), tensor: 2 (over y).
Axes of the slice: x: 2, y: 2, z: 4, core: 2. Of those that a mesh axis runs over, the one named last changes fastest.
Arguments:
- tokens: bfloat16 [3072, 1536], P('dp'), may hold values from -6 to 6
- prefix: int32 [16], P('dp'), may hold values from 19 to 96
- g_attn: bfloat16 [1536], P('dp'), may hold values from 0.5 to 1.5
- w_query: bfloat16 [128, 12, 1536], P('dp', 'tensor'), may hold values from -0.15625 to 0.15625
- b_query: bfloat16 [128, 12], P('dp', 'tensor'), may hold values from -3 to 3
- w_key: bfloat16 [128, 2, 1536], P('dp', 'tensor'), may hold values from -0.15625 to 0.15625
- b_key: bfloat16 [128, 2], P(None, 'tensor'), may hold values from -3 to 3
- w_value: bfloat16 [128, 2, 1536], P('dp', 'tensor'), may hold values from -0.15625 to 0.15625
- b_value: bfloat16 [128, 2], P('dp', 'tensor'), may hold values from -3 to 3
- w_out: bfloat16 [128, 12, 1536], P('dp', 'tensor'), may hold values from -0.75 to 0.75
- g_mlp: bfloat16 [1536], P('dp'), may hold values from 0.5 to 1.5
- w_gate: bfloat16 [8960, 1536], P(('dp', 'tensor')), may hold values from -0.15625 to 0.15625
- w_up: bfloat16 [8960, 1536], P(('dp', 'tensor')), may hold values from -0.15625 to 0.15625
- w_down: bfloat16 [8960, 1536], P(('dp', 'tensor')), may hold values from -0.0625 to 0.0625
- cotangent: bfloat16 [3072, 1536], P('dp'), may hold values from -6 to 6
Outputs:
- out_tokens: bfloat16 [3072, 1536], P('dp')
- grad_tokens: float32 [3072, 1536], P('dp')
- grad_gattn: float32 [1536], P('dp')
- grad_wquery: float32 [128, 12, 1536], P('dp', 'tensor')
- grad_bquery: float32 [128, 12], P('dp', 'tensor')
- grad_wkey: float32 [128, 2, 1536], P('dp', 'tensor')
- grad_bkey: float32 [128, 2], P(None, 'tensor')
- grad_wvalue: float32 [128, 2, 1536], P('dp', 'tensor')
- grad_bvalue: float32 [128, 2], P('dp', 'tensor')
- grad_wout: float32 [128, 12, 1536], P('dp', 'tensor')
- grad_gmlp: float32 [1536], P('dp')
- grad_wgate: float32 [8960, 1536], P(('dp', 'tensor'))
- grad_wup: float32 [8960, 1536], P(('dp', 'tensor'))
- grad_wdown: float32 [8960, 1536], P(('dp', 'tensor'))
All inputs are finite; a program needn't handle non-finite values.
Results may differ from a plain program's by a relative error of at most 0.022.
Values may be sent and summed in bfloat16 or wider, within the bound.
A program may use at most 256 MiB of HBM per device.

v0:
```python
import functools

import jax
import jax.numpy as jnp
import numpy as np
from jax import lax
from jax.experimental import pallas as pl
from jax.experimental.pallas import tpu as pltpu
from jax.sharding import PartitionSpec as P

EPS = 1e-06
ROPE_BASE = 1000000.0
NEG_BIG = -1e30


def rotate(field, flip_sign):
    half_dim = field.shape[-1] // 2
    places = jnp.arange(field.shape[0], dtype=jnp.float32)
    freqs = ROPE_BASE ** (-(jnp.arange(half_dim, dtype=jnp.float32) * 2.0 / field.shape[-1]))
    angles = places[:, None] * freqs[None, :]
    cosine = jnp.cos(angles)[:, None, :]
    sine = flip_sign * jnp.sin(angles)[:, None, :]
    first = field[..., :half_dim]
    second = field[..., half_dim:]
    return jnp.concatenate(
        [first * cosine - second * sine, second * cosine + first * sine], axis=-1
    )


def normed(field, gain):
    return field * lax.rsqrt(jnp.mean(field * field, axis=-1, keepdims=True) + EPS) * gain


def whole_gather(
    tokens,
    prefix,
    g_attn,
    w_query,
    b_query,
    w_key,
    b_key,
    w_value,
    b_value,
    w_out,
    g_mlp,
    w_gate,
    w_up,
    w_down,
    cotangent,
):
    gain_one, query_w, query_b, key_w, value_w, value_b, out_w = (
        lax.all_gather(g_attn, "dp", axis=0, tiled=True),
        lax.all_gather(w_query, "dp", axis=0, tiled=True),
        lax.all_gather(b_query, "dp", axis=0, tiled=True),
        lax.all_gather(w_key, "dp", axis=0, tiled=True),
        lax.all_gather(w_value, "dp", axis=0, tiled=True),
        lax.all_gather(b_value, "dp", axis=0, tiled=True),
        lax.all_gather(w_out, "dp", axis=0, tiled=True),
    )
    tok_float = tokens.astype(jnp.float32)
    gain_in = gain_one.astype(jnp.float32)
    normed_in = normed(tok_float, gain_in).astype(jnp.bfloat16)
    query_pre = (
        jnp.einsum("sd,ehd->she", normed_in, query_w, preferred_element_type=jnp.float32)
        + query_b.astype(jnp.float32).T
    )
    key_pre = (
        jnp.einsum("sd,ehd->she", normed_in, key_w, preferred_element_type=jnp.float32)
        + b_key.astype(jnp.float32).T
    )
    value_pre = (
        jnp.einsum("sd,ehd->she", normed_in, value_w, preferred_element_type=jnp.float32)
        + value_b.astype(jnp.float32).T
    )
    seq_len, heads_local, head_dim = query_pre.shape
    kv_local = key_pre.shape[1]
    group_size = heads_local // kv_local
    score_scale = head_dim ** (-0.5)
    query_rot = (
        rotate(query_pre, 1.0).astype(jnp.bfloat16).reshape(seq_len, kv_local, group_size, head_dim)
    )
    key_rot = rotate(key_pre, 1.0).astype(jnp.bfloat16)
    value_low = value_pre.astype(jnp.bfloat16)
    row_index = lax.broadcasted_iota(jnp.int32, (seq_len, seq_len), 0)
    col_index = lax.broadcasted_iota(jnp.int32, (seq_len, seq_len), 1)
    allowed = (col_index <= row_index) | (col_index < prefix[0])

    def score_of():
        raw_scores = (
            jnp.einsum("skgd,tkd->kgst", query_rot, key_rot, preferred_element_type=jnp.float32)
            * score_scale
        )
        return jnp.where(allowed, raw_scores, NEG_BIG)

    scores = score_of()
    row_peak = jnp.max(scores, axis=-1, keepdims=True)
    shifted_exp = jnp.exp(scores - row_peak)
    row_total = jnp.sum(shifted_exp, axis=-1, keepdims=True)
    probs_low = (shifted_exp / row_total).astype(jnp.bfloat16)
    log_total = row_peak + jnp.log(row_total)
    attended = jnp.einsum(
        "kgst,tkd->skgd", probs_low, value_low, preferred_element_type=jnp.float32
    )
    attended_low = attended.reshape(seq_len, heads_local, head_dim).astype(jnp.bfloat16)
    attn_part = jnp.einsum("she,ehd->sd", attended_low, out_w, preferred_element_type=jnp.float32)
    middle = tok_float + lax.psum(attn_part, "tensor")
    gain_two, gate_w, up_w, down_w = (
        lax.all_gather(g_mlp, "dp", axis=0, tiled=True),
        lax.all_gather(w_gate, "dp", axis=0, tiled=True),
        lax.all_gather(w_up, "dp", axis=0, tiled=True),
        lax.all_gather(w_down, "dp", axis=0, tiled=True),
    )
    gain_mid = gain_two.astype(jnp.float32)
    normed_mid = normed(middle, gain_mid).astype(jnp.bfloat16)
    contract = (((1,), (1,)), ((), ()))
    rows_first = (((0,), (0,)), ((), ()))
    gate_val = lax.dot_general(normed_mid, gate_w, contract, preferred_element_type=jnp.float32)
    up_val = lax.dot_general(normed_mid, up_w, contract, preferred_element_type=jnp.float32)
    sigmoid_gate = jax.nn.sigmoid(gate_val)
    silu_gate = gate_val * sigmoid_gate
    hidden = (silu_gate * up_val).astype(jnp.bfloat16)
    mlp_part = jnp.dot(hidden, down_w, preferred_element_type=jnp.float32)
    result = middle + lax.psum(mlp_part.astype(jnp.bfloat16), "tensor").astype(jnp.float32)
    out_tokens = result.astype(jnp.bfloat16)
    gain_two, gate_w, up_w, down_w = (
        lax.all_gather(g_mlp, "dp", axis=0, tiled=True),
        lax.all_gather(w_gate, "dp", axis=0, tiled=True),
        lax.all_gather(w_up, "dp", axis=0, tiled=True),
        lax.all_gather(w_down, "dp", axis=0, tiled=True),
    )
    cot_float = cotangent.astype(jnp.float32)
    grad_wdown = lax.dot_general(hidden, cotangent, rows_first, preferred_element_type=jnp.float32)
    grad_hidden = lax.dot_general(cotangent, down_w, contract, preferred_element_type=jnp.float32)
    grad_gate = (
        grad_hidden * up_val * sigmoid_gate * (1.0 + gate_val * (1.0 - sigmoid_gate))
    ).astype(jnp.bfloat16)
    grad_up = (grad_hidden * silu_gate).astype(jnp.bfloat16)
    grad_wgate = lax.dot_general(
        grad_gate, normed_mid, rows_first, preferred_element_type=jnp.float32
    )
    grad_wup = lax.dot_general(grad_up, normed_mid, rows_first, preferred_element_type=jnp.float32)
    mid_part = jnp.dot(grad_gate, gate_w, preferred_element_type=jnp.float32) + jnp.dot(
        grad_up, up_w, preferred_element_type=jnp.float32
    )
    grad_normed_mid = lax.psum(mid_part, "tensor")
    unused_mid, pull_mid = jax.vjp(normed, middle, gain_mid)
    grad_mid_norm, grad_gmlp = pull_mid(grad_normed_mid)
    grad_middle = cot_float + grad_mid_norm
    gain_one, query_w, query_b, key_w, value_w, value_b, out_w = (
        lax.all_gather(g_attn, "dp", axis=0, tiled=True),
        lax.all_gather(w_query, "dp", axis=0, tiled=True),
        lax.all_gather(b_query, "dp", axis=0, tiled=True),
        lax.all_gather(w_key, "dp", axis=0, tiled=True),
        lax.all_gather(w_value, "dp", axis=0, tiled=True),
        lax.all_gather(b_value, "dp", axis=0, tiled=True),
        lax.all_gather(w_out, "dp", axis=0, tiled=True),
    )
    middle_low = grad_middle.astype(jnp.bfloat16)
    grad_wout = jnp.einsum(
        "she,sd->ehd", attended_low, middle_low, preferred_element_type=jnp.float32
    )
    grad_attended = (
        jnp.einsum("sd,ehd->she", middle_low, out_w, preferred_element_type=jnp.float32)
        .astype(jnp.bfloat16)
        .reshape(seq_len, kv_local, group_size, head_dim)
    )
    probs_again = jnp.exp(score_of() - log_total)
    again_low = probs_again.astype(jnp.bfloat16)
    grad_value = jnp.einsum(
        "kgst,skgd->tkd", again_low, grad_attended, preferred_element_type=jnp.float32
    ).astype(jnp.bfloat16)
    grad_probs = jnp.einsum(
        "skgd,tkd->kgst", grad_attended, value_low, preferred_element_type=jnp.float32
    )
    inner_sum = jnp.sum(probs_again * grad_probs, axis=-1, keepdims=True)
    grad_scores = (probs_again * (grad_probs - inner_sum)).astype(jnp.bfloat16)
    grad_qrot = (
        jnp.einsum(
            "kgst,tkd->skgd", grad_scores, key_rot, preferred_element_type=jnp.float32
        ).reshape(seq_len, heads_local, head_dim)
        * score_scale
    )
    grad_krot = (
        jnp.einsum("kgst,skgd->tkd", grad_scores, query_rot, preferred_element_type=jnp.float32)
        * score_scale
    )
    grad_query = rotate(grad_qrot, -1.0).astype(jnp.bfloat16)
    grad_key = rotate(grad_krot, -1.0).astype(jnp.bfloat16)
    grad_wquery = jnp.einsum(
        "she,sd->ehd", grad_query, normed_in, preferred_element_type=jnp.float32
    )
    grad_bquery = jnp.sum(grad_query.astype(jnp.float32), axis=0).T
    grad_wkey = jnp.einsum("she,sd->ehd", grad_key, normed_in, preferred_element_type=jnp.float32)
    grad_bkey = jnp.sum(grad_key.astype(jnp.float32), axis=0).T
    key_bias_total = lax.psum(grad_bkey, "dp")
    grad_wvalue = jnp.einsum(
        "she,sd->ehd", grad_value, normed_in, preferred_element_type=jnp.float32
    )
    grad_bvalue = jnp.sum(grad_value.astype(jnp.float32), axis=0).T
    in_part = jnp.einsum("she,ehd->sd", grad_query, query_w, preferred_element_type=jnp.float32)
    in_part = in_part + jnp.einsum(
        "she,ehd->sd", grad_key, key_w, preferred_element_type=jnp.float32
    )
    in_part = in_part + jnp.einsum(
        "she,ehd->sd", grad_value, value_w, preferred_element_type=jnp.float32
    )
    grad_normed_in = lax.psum(in_part.astype(jnp.bfloat16), "tensor").astype(jnp.float32)
    unused_in, pull_in = jax.vjp(normed, tok_float, gain_in)
    grad_in_norm, grad_gattn = pull_in(grad_normed_in)
    grad_tokens = grad_middle + grad_in_norm
    every_sum = (
        lax.psum_scatter(grad_gattn, "dp", scatter_dimension=0, tiled=True),
        lax.psum_scatter(grad_wquery, "dp", scatter_dimension=0, tiled=True),
        lax.psum_scatter(grad_bquery, "dp", scatter_dimension=0, tiled=True),
        lax.psum_scatter(grad_wkey, "dp", scatter_dimension=0, tiled=True),
        lax.psum_scatter(grad_wvalue, "dp", scatter_dimension=0, tiled=True),
        lax.psum_scatter(grad_bvalue, "dp", scatter_dimension=0, tiled=True),
        lax.psum_scatter(grad_wout, "dp", scatter_dimension=0, tiled=True),
        lax.psum_scatter(grad_gmlp, "dp", scatter_dimension=0, tiled=True),
        lax.psum_scatter(grad_wgate, "dp", scatter_dimension=0, tiled=True),
        lax.psum_scatter(grad_wup, "dp", scatter_dimension=0, tiled=True),
        lax.psum_scatter(grad_wdown, "dp", scatter_dimension=0, tiled=True),
    )
    attn_grads = every_sum[:7]
    mlp_grads = every_sum[7:]
    return (
        out_tokens,
        grad_tokens,
        attn_grads[0],
        attn_grads[1],
        attn_grads[2],
        attn_grads[3],
        key_bias_total,
        attn_grads[4],
        attn_grads[5],
        attn_grads[6],
        mlp_grads[0],
        mlp_grads[1],
        mlp_grads[2],
        mlp_grads[3],
    )


MESH = pl.DeviceIdType.MESH
BF = jnp.bfloat16
F32 = jnp.float32
NT = (((1,), (1,)), ((), ()))
NN = (((1,), (0,)), ((), ()))
TN = (((0,), (0,)), ((), ()))
VMEM_LIMIT = 67043328
ANY = pl.BlockSpec(memory_space=pl.ANY)
VM = pl.BlockSpec(memory_space=pltpu.VMEM)


def dot(a, b, dims):
    return lax.dot_general(a, b, dims, preferred_element_type=F32)


class Spot:
    def __init__(self, nz):
        self.nz = nz
        self.dp = lax.axis_index("dp")
        self.t = lax.axis_index("tensor")
        self.z, self.x, self.c = self.dp // 4, (self.dp // 2) % 2, self.dp % 2
        self.xn = (self.index(self.z, 1 - self.x, self.c), self.t)
        self.cn = (self.index(self.z, self.x, 1 - self.c), self.t)
        self.yn = (self.dp, 1 - self.t)

    def index(self, z, x, c):
        return (z * 2 + x) * 2 + c

    def near(self, k):
        nz, z = self.nz, self.z
        edge = jnp.minimum(z, nz - 1 - z)
        side = jnp.where(z <= nz - 1 - z, -1, 1)
        half = (k + 1) // 2
        close = side * half if k % 2 else -side * half
        return z + jnp.where(k <= 2 * edge, close, -side * (k - edge))

    def step(self, way):
        z = jnp.clip(self.z + way, 0, self.nz - 1)
        return (self.index(z, self.x, self.c), self.t)


class Wires:
    def __init__(self):
        self.sent = []

    def send(self, src, dst, send_sem, recv_sem, device, only=None):
        copy = pltpu.make_async_remote_copy(
            src_ref=src,
            dst_ref=dst,
            send_sem=send_sem,
            recv_sem=recv_sem,
            device_id=device,
            device_id_type=MESH,
        )
        if only is None:
            copy.start()
        else:
            pl.when(only)(copy.start)
        self.sent.append((copy, only))

    def landed(self, dst, recv_sem, spot):
        pltpu.make_async_remote_copy(
            src_ref=dst,
            dst_ref=dst,
            send_sem=recv_sem,
            recv_sem=recv_sem,
            device_id=spot.xn,
            device_id_type=MESH,
        ).wait_recv()

    def drain(self):
        for copy, only in self.sent:
            if only is None:
                copy.wait_send()
            else:
                pl.when(only)(copy.wait_send)
        self.sent = []


class Gather:
    def __init__(self, at, wires, slot, recv, send, core=None):
        self.at, self.wires, self.slot, self.recv, self.send, self.core = at, wires, slot, recv, send, core

    def hand(self, src, z, x, lane, device, only=None):
        self.wires.send(src, self.slot(z, x), self.send.at[lane], self.recv.at[z, x], device, only)

    def to_core(self, src, z, x, lane, only=None):
        if self.core is not None:
            slot, recv, send = self.core
            self.wires.send(src, slot(z, x), send.at[lane], recv.at[z, x], self.at.cn, only)

    def start(self, src):
        at = self.at
        self.hand(src, at.z, at.x, 0, at.step(1), at.z < at.nz - 1)
        self.hand(src, at.z, at.x, 1, at.step(-1), at.z > 0)
        self.hand(src, at.z, at.x, 2, at.xn)
        self.to_core(src, at.z, at.x, 0)

    def relay(self, k):
        at = self.at
        for side, way in ((0, 1), (1, -1)):
            z = at.z - way * k
            real = (z >= 0) & (z < at.nz)
            block = self.slot(z, at.x)
            pl.when(real)(functools.partial(self.wires.landed, block, self.recv.at[z, at.x], at))
            lane = 3 * k + side * 3 * (at.nz - 1)
            ahead = at.z + way
            self.hand(block, z, at.x, lane, at.step(way), real & (ahead >= 0) & (ahead < at.nz))
            self.hand(block, z, at.x, lane + 1, at.xn, real)
            self.to_core(block, z, at.x, k + side * (at.nz - 1), real)

    def column(self, k):
        at = self.at
        z = at.near(k)
        block = self.slot(z, 1 - at.x)
        self.wires.landed(block, self.recv.at[z, 1 - at.x], at)
        self.to_core(block, z, 1 - at.x, 2 * at.nz - 1 + k)

    @staticmethod
    def lanes(nz):
        return 3 + 6 * (nz - 1)

    @staticmethod
    def core_lanes(nz):
        return 3 * nz - 1


class LineSum:
    def __init__(self, at, wires, inbox, outbox, recv, send):
        self.at, self.wires, self.inbox, self.outbox, self.recv, self.send = at, wires, inbox, outbox, recv, send

    def add(self, way, s, acc_ref, real):
        at = self.at

        def go():
            self.wires.landed(self.inbox.at[way, s], self.recv.at[way, s], at)
            acc_ref[...] += self.inbox[way, s].astype(F32)

        pl.when(real)(go)

    def push(self, k, acc_ref, only=None, again=False):
        at = self.at
        s = at.near(k)
        up = s > at.z
        way = jnp.where(up, 0, 1)
        target = at.step(jnp.where(up, 1, -1))

        def fill():
            self.add(way, s, acc_ref, (up & (at.z > 0)) | ((s < at.z) & (at.z < at.nz - 1)))
            self.outbox[k] = acc_ref[...].astype(BF)

        fill() if only is None else pl.when(only)(fill)
        self.wires.send(
            self.outbox.at[k], self.inbox.at[way, s], self.send.at[k], self.recv.at[way, s], target, only
        )
        if only is not None:
            copy, _ = self.wires.sent.pop()
            if not again:
                self.wires.sent.append((copy, None))

    def close(self, acc_ref):
        at = self.at
        self.add(0, at.z, acc_ref, at.z > 0)
        self.add(1, at.z, acc_ref, at.z < at.nz - 1)


class OwnerSum:
    def __init__(self, at, wires, full, rows, bufs, sems):
        self.at, self.wires, self.full, self.rows = at, wires, full, rows
        self.core_out, self.core_in, self.x_out, self.x_in, outbox, inbox, self.acc = bufs
        self.a_recv, self.a_send, self.x_recv, self.x_send, z_recv, z_send = sems
        self.line = LineSum(at, wires, inbox, outbox, z_recv, z_send)
        self.order = list(range(at.nz - 1, -1, -1))

    @staticmethod
    def buffers(nz, units, rows, wide):
        block = (units * rows, wide)
        vm = pltpu.VMEM
        return [
            vm((nz, 2) + block, BF),
            vm((nz, 2) + block, BF),
            vm((nz,) + block, BF),
            vm((nz,) + block, BF),
            vm((nz,) + block, BF),
            vm((2, nz) + block, BF),
            vm(block, F32),
        ]

    @staticmethod
    def semaphores(nz):
        dma = pltpu.SemaphoreType.DMA
        return [dma((nz, 2)), dma((nz, 2)), dma((nz,)), dma((nz,)), dma((2, nz)), dma((nz,))]

    def terms(self, z, x, c):
        start = pl.multiple_of(self.at.index(z, x, c) * self.rows, self.rows)
        piece = self.full[:, pl.ds(start, self.rows), :]
        return piece.reshape(piece.shape[0] * self.rows, piece.shape[2])

    def to_core(self):
        at = self.at
        for far in (1, 0):
            for k in self.order:
                x = 1 - at.x if far else at.x
                self.core_out[k, far] = self.terms(at.near(k), x, 1 - at.c).astype(BF)
                self.wires.send(
                    self.core_out.at[k, far],
                    self.core_in.at[k, far],
                    self.a_send.at[k, far],
                    self.a_recv.at[k, far],
                    at.cn,
                )

    def across(self):
        at = self.at
        for k in self.order:
            self.wires.landed(self.core_in.at[k, 1], self.a_recv.at[k, 1], at)
            both = self.terms(at.near(k), 1 - at.x, at.c) + self.core_in[k, 1].astype(F32)
            self.x_out[k] = both.astype(BF)
            self.wires.send(self.x_out.at[k], self.x_in.at[k], self.x_send.at[k], self.x_recv.at[k], at.xn)

    def along(self, out):
        at = self.at
        for k in self.order:
            self.wires.landed(self.core_in.at[k, 0], self.a_recv.at[k, 0], at)
            self.wires.landed(self.x_in.at[k], self.x_recv.at[k], at)
            acc = self.acc if k else out
            acc[...] = (
                self.terms(at.near(k), at.x, at.c)
                + self.core_in[k, 0].astype(F32)
                + self.x_in[k].astype(F32)
            )
            if k:
                self.line.push(k, acc)

    def close(self, out):
        self.line.close(out)


def greet(at, devices, line=True):
    barrier = pltpu.get_barrier_semaphore()

    def hello(device):
        pl.semaphore_signal(barrier, inc=1, device_id=device, device_id_type=MESH)

    for device in devices:
        hello(device)
    count = len(devices)
    if line:
        up, down = at.z < at.nz - 1, at.z > 0
        pl.when(up)(functools.partial(hello, at.step(1)))
        pl.when(down)(functools.partial(hello, at.step(-1)))
        count = count + jnp.where(up, 1, 0) + jnp.where(down, 1, 0)
    pl.semaphore_wait(barrier, count)


def gather_kernel(
    nz,
    qkv_in,
    wo_in,
    small_in,
    cot_in,
    gate_in,
    up_in,
    down_in,
    qkv,
    wo,
    small,
    cot,
    mlp_w,
    stage_a,
    stage_b,
    stage_c,
    local_sem,
    q_recv,
    q_send,
    q_core_recv,
    q_core_send,
    o_recv,
    o_send,
    o_core_recv,
    o_core_send,
    s_recv,
    s_send,
    c_recv,
    c_send,
    w_recv,
    w_send,
):
    at = Spot(nz)
    ndp = 4 * nz
    half = cot_in.shape[0] // 2
    rows = qkv_in.shape[1]
    others = [(lax.rem(at.dp + p, ndp), at.t) for p in range(1, ndp)]
    greet(at, others + [at.yn], line=False)
    wires = Wires()

    def part(ref, core):
        def slot(z, x):
            owner = at.index(z, x, core)
            return ref.at[:, pl.ds(pl.multiple_of(owner * rows, rows), rows), :]

        return slot

    def cot_slot(z, x):
        return cot.at[z, x]

    q_slot, o_slot = part(qkv, at.c), part(wo, at.c)
    gq = Gather(at, wires, q_slot, q_recv, q_send, (q_slot, q_core_recv, q_core_send))
    go = Gather(at, wires, o_slot, o_recv, o_send, (o_slot, o_core_recv, o_core_send))
    gc = Gather(at, wires, cot_slot, c_recv, c_send)
    gq.start(qkv_in)
    go.start(wo_in)
    mine = at.c * 2 + at.t
    for i, src in enumerate((gate_in, up_in, down_in)):
        wires.send(src, mlp_w.at[i, mine], w_send.at[0, i], w_recv.at[i, mine], at.yn)
        wires.send(src, mlp_w.at[i, mine], w_send.at[1, i], w_recv.at[i, mine], at.cn)
    for p, device in enumerate(others):
        wires.send(small_in, small.at[at.dp], s_send.at[p], s_recv.at[at.dp], device)
    loads = [
        pltpu.make_async_copy(qkv_in, stage_a, local_sem.at[0]),
        pltpu.make_async_copy(wo_in, stage_b, local_sem.at[1]),
        pltpu.make_async_copy(small_in, stage_c, local_sem.at[2]),
    ]
    stores = [
        pltpu.make_async_copy(stage_a, q_slot(at.z, at.x), local_sem.at[3]),
        pltpu.make_async_copy(stage_b, o_slot(at.z, at.x), local_sem.at[4]),
        pltpu.make_async_copy(stage_c, small.at[at.dp], local_sem.at[5]),
    ]
    for load in loads:
        load.start()
    for load, store in zip(loads, stores):
        load.wait()
        store.start()
    for k in range(1, nz):
        gq.relay(k)
        go.relay(k)
    gc.start(cot_in.at[pl.ds(pl.multiple_of(at.t * half, half), half), :])
    for k in range(nz):
        gq.column(k)
        go.column(k)
    for k in range(1, nz):
        gc.relay(k)
    for k in range(nz):
        gc.column(k)
    across = at.c * 2 + 1 - at.t
    for i in range(3):
        wires.landed(mlp_w.at[i, across], w_recv.at[i, across], at)
        wires.send(mlp_w.at[i, across], mlp_w.at[i, across], w_send.at[2, i], w_recv.at[i, across], at.cn)
    for i in range(3):
        for tt in range(2):
            there = (1 - at.c) * 2 + tt
            wires.landed(mlp_w.at[i, there], w_recv.at[i, there], at)
    for device in others:
        wires.landed(small.at[device[0]], s_recv.at[device[0]], at)
    for ref, recv in ((qkv, q_core_recv), (wo, o_core_recv)):
        slot = part(ref, 1 - at.c)
        for z in range(nz):
            for x in range(2):
                wires.landed(slot(z, x), recv.at[z, x], at)
    for store in stores:
        store.wait()
    wires.drain()


def gather_weights(nz, qkv, wo, small, cotangent, gate, up, down):
    ndp = 4 * nz
    half, wide = cotangent.shape[0] // 2, cotangent.shape[1]
    shape = jax.ShapeDtypeStruct
    dma = pltpu.SemaphoreType.DMA
    return pl.pallas_call(
        functools.partial(gather_kernel, nz),
        out_shape=(
            shape((qkv.shape[0], ndp * qkv.shape[1], wide), BF),
            shape((wo.shape[0], ndp * wo.shape[1], wide), BF),
            shape((ndp,) + small.shape, BF),
            shape((nz, 2, half, wide), BF),
            shape((3, 4) + gate.shape, BF),
        ),
        in_specs=[ANY] * 7,
        out_specs=[ANY] * 5,
        scratch_shapes=[
            pltpu.VMEM(qkv.shape, BF),
            pltpu.VMEM(wo.shape, BF),
            pltpu.VMEM(small.shape, BF),
            dma((6,)),
            dma((nz, 2)),
            dma((Gather.lanes(nz),)),
            dma((nz, 2)),
            dma((Gather.core_lanes(nz),)),
            dma((nz, 2)),
            dma((Gather.lanes(nz),)),
            dma((nz, 2)),
            dma((Gather.core_lanes(nz),)),
            dma((ndp,)),
            dma((ndp,)),
            dma((nz, 2)),
            dma((Gather.lanes(nz),)),
            dma((3, 4)),
            dma((3, 3)),
        ],
        compiler_params=pltpu.CompilerParams(
            collective_id=1, has_side_effects=True, vmem_limit_bytes=VMEM_LIMIT
        ),
        name="gather_weights",
    )(qkv, wo, small, cotangent, gate, up, down)


def mlp_kernel(
    nz,
    tok_in,
    part_in,
    gain_in,
    cot_in,
    mlp_in,
    cot_own_in,
    gate_in,
    up_in,
    down_in,
    out_part,
    keep_gate,
    keep_up,
    keep_down,
    give,
    grad_half,
    mid_half,
    gain_send,
    weights,
    cot,
    nm,
    gh,
    hid,
    gg,
    gu,
    own,
    xs,
    xr,
    z_in,
    pair,
    grads,
    partner,
    ysend,
    yrecv,
    down_send,
    down_recv,
    local_sem,
    n_recv,
    n_send,
    x_recv,
    x_send,
    z_recv,
    z_send,
    p_recv,
    p_send,
    y_recv,
    y_send,
):
    at = Spot(nz)
    half, wide = nm.shape[2], nm.shape[3]
    two = 2 * half
    shard = mlp_in.shape[2]
    padded = weights.shape[2]
    units = 4 * padded
    wires = Wires()
    mine = at.c * 2 + at.t

    loads = []

    def load(src, dst, sem):
        copy = pltpu.make_async_copy(src, dst, sem)
        copy.start()
        loads.append(copy)
        return copy

    per = [[], [], []]
    for i, src in ((2, down_in), (0, gate_in), (1, up_in)):
        per[i].append(load(src, weights.at[i, mine, pl.ds(0, shard)], local_sem.at[i * 4]))
        for j, slot in enumerate((at.c * 2 + 1 - at.t, (1 - at.c) * 2, (1 - at.c) * 2 + 1)):
            per[i].append(
                load(mlp_in.at[i, slot], weights.at[i, slot, pl.ds(0, shard)], local_sem.at[i * 4 + 1 + j])
            )
    cot_loads = [
        load(
            cot_own_in.at[pl.ds(pl.multiple_of(at.t * half, half), half), :],
            cot.at[at.z, at.x],
            local_sem.at[12],
        )
    ]
    for k in range(nz):
        zk = at.near(k)
        if k:
            cot_loads.append(load(cot_in.at[zk, at.x], cot.at[zk, at.x], local_sem.at[12 + 2 * k]))
        cot_loads.append(load(cot_in.at[zk, 1 - at.x], cot.at[zk, 1 - at.x], local_sem.at[13 + 2 * k]))
    for i in range(3):
        for s in range(4):
            weights[i, s, shard:padded, :] = jnp.zeros((padded - shard, wide), BF)

    far_row = pl.multiple_of((1 - at.t) * half, half)
    own_row = pl.multiple_of(at.t * half, half)
    greet(at, [at.xn, at.yn, at.cn])
    ysend[...] = part_in[pl.ds(far_row, half), :].astype(BF)
    wires.send(ysend, yrecv, y_send.at[0], y_recv.at[0], at.yn)
    for copy in per[2] + cot_loads:
        copy.wait()
    down_w = weights.at[2]

    for k in range(nz):
        zk = at.near(k)
        gh[zk] = dot(cot[zk].reshape(two, wide), down_w[...].reshape(units, wide), NT)

    wires.landed(yrecv, y_recv.at[0], at)
    middle = (
        tok_in[pl.ds(own_row, half), :].astype(F32)
        + part_in[pl.ds(own_row, half), :]
        + yrecv[...].astype(F32)
    )
    gain = gain_in[...]
    rms = lax.rsqrt(jnp.mean(middle * middle, axis=-1, keepdims=True) + EPS)
    mid_half[...] = middle
    nm[at.z, at.x] = (middle * rms * gain).astype(BF)

    def nm_slot(z, x):
        return nm.at[z, x]

    gather = Gather(at, wires, nm_slot, n_recv, n_send)
    line = LineSum(at, wires, z_in, xr, z_recv, z_send)
    at_end = (at.z == 0) | (at.z == nz - 1)
    gather.start(nm.at[at.z, at.x])
    for copy in per[0] + per[1]:
        copy.wait()
    gate_w, up_w = weights.at[0], weights.at[1]

    def hand_over(k):
        wires.send(xs.at[k], xr.at[k], x_send.at[k], x_recv.at[k], at.xn)

    def column_sum(k):
        wires.landed(xr.at[k], x_recv.at[k], at)
        own[k] += xr[k].astype(F32)
        if k:
            line.push(k, own.at[k], only=at_end)

    if nz > 1:
        gather.relay(1)
    for k in range(nz):
        zk = at.near(k)
        gather.column(k)
        a = nm[zk].reshape(two, wide)
        gate = dot(a, gate_w[...].reshape(units, wide), NT)
        up = dot(a, up_w[...].reshape(units, wide), NT)
        sig = jax.nn.sigmoid(gate)
        silu = gate * sig
        hid[zk] = (silu * up).astype(BF)
        ghk = gh[zk]
        gg[zk] = (ghk * up * sig * (1.0 + gate * (1.0 - sig))).astype(BF)
        gu[zk] = (ghk * silu).astype(BF)
        if k + 2 < nz:
            gather.relay(k + 2)
        pair[...] = (
            dot(gg[zk], gate_w[...].reshape(units, wide), NN)
            + dot(gu[zk], up_w[...].reshape(units, wide), NN)
        ).reshape(2, half, wide)
        xs[k] = pair[1 - at.x].astype(BF)
        own[k] = pair[at.x]
        if k:
            hand_over(k)
        if k > 1:
            column_sum(k - 1)
    hand_over(0)
    tile = 512

    def weight_grad(i, lhs, rhs):
        left = lhs[...].reshape(nz * two, units)
        for j in range(wide // tile):
            cols = slice(j * tile, (j + 1) * tile)
            right = rhs[:, :, :, cols].reshape(nz * two, tile)
            acc = dot(left, right, TN).astype(BF).reshape(4, padded, tile)
            grads[i, :, :, cols] = acc[:, :shard]
        for j in range(2):
            wires.send(
                grads.at[i, (1 - at.c) * 2 + j], partner.at[i, j], p_send.at[i, j], p_recv.at[i, j], at.cn
            )

    def chip_sum(i, kept, given):
        for j in range(2):
            wires.landed(partner.at[i, j], p_recv.at[i, j], at)
        kept[...] = grads[i, mine].astype(F32) + partner[i, at.t].astype(F32)
        given[...] = (
            grads[i, at.c * 2 + 1 - at.t].astype(F32) + partner[i, 1 - at.t].astype(F32)
        ).astype(BF)

    weight_grad(2, hid, cot)
    for k in range(nz):
        zk = at.near(k)
        out_part[zk] = dot(hid[zk], down_w[...].reshape(units, wide), NN).astype(BF).reshape(2, half, wide)
    chip_sum(2, keep_down, down_send)
    wires.send(down_send, down_recv, y_send.at[1], y_recv.at[1], at.yn)
    column_sum(nz - 1)
    for k in [nz - 2, nz - 1] + list(range(nz - 3, 0, -1)):
        line.push(k, own.at[k], only=jnp.logical_not(at_end), again=True)
    weight_grad(0, gg, nm)
    weight_grad(1, gu, nm)
    column_sum(0)
    line.close(own.at[0])
    total = own[0]
    middle = mid_half[...]
    rms = lax.rsqrt(jnp.mean(middle * middle, axis=-1, keepdims=True) + EPS)
    unit = middle * rms
    gain_send[...] = jnp.sum(total * unit, axis=0, keepdims=True)
    scaled = total * gain
    cot_f = cot[at.z, at.x].astype(F32)
    grad_mid = cot_f + rms * (scaled - unit * jnp.mean(scaled * unit, axis=-1, keepdims=True))
    grad_half[...] = grad_mid.astype(BF)
    chip_sum(0, keep_gate, give.at[0])
    chip_sum(1, keep_up, give.at[1])
    wires.landed(down_recv, y_recv.at[1], at)
    keep_down[...] += down_recv[...].astype(F32)
    wires.drain()


def mlp_step(nz, tokens, part, gain, cot_all, mlp_all, cotangent, gate, up, down):
    half, wide = cotangent.shape[0] // 2, cotangent.shape[1]
    shard = gate.shape[0]
    padded = -(-shard // 32) * 32
    units = 4 * padded
    shape = jax.ShapeDtypeStruct
    dma = pltpu.SemaphoreType.DMA
    vm = pltpu.VMEM
    return pl.pallas_call(
        functools.partial(mlp_kernel, nz),
        out_shape=(
            shape((nz, 2, half, wide), BF),
            shape((shard, wide), F32),
            shape((shard, wide), F32),
            shape((shard, wide), F32),
            shape((2, shard, wide), BF),
            shape((half, wide), BF),
            shape((half, wide), F32),
            shape((1, wide), F32),
        ),
        in_specs=[VM, VM, VM] + [ANY] * 6,
        out_specs=[VM] * 8,
        scratch_shapes=[
            vm((3, 4, padded, wide), BF),
            vm((nz, 2, half, wide), BF),
            vm((nz, 2, half, wide), BF),
            vm((nz, 2 * half, units), F32),
            vm((nz, 2 * half, units), BF),
            vm((nz, 2 * half, units), BF),
            vm((nz, 2 * half, units), BF),
            vm((nz, half, wide), F32),
            vm((nz, half, wide), BF),
            vm((nz, half, wide), BF),
            vm((2, nz, half, wide), BF),
            vm((2, half, wide), F32),
            vm((3, 4, shard, wide), BF),
            vm((3, 2, shard, wide), BF),
            vm((half, wide), BF),
            vm((half, wide), BF),
            vm((shard, wide), BF),
            vm((shard, wide), BF),
            dma((12 + 2 * nz + 2,)),
            dma((nz, 2)),
            dma((Gather.lanes(nz),)),
            dma((nz,)),
            dma((nz,)),
            dma((2, nz)),
            dma((nz,)),
            dma((3, 2)),
            dma((3, 2)),
            dma((2,)),
            dma((2,)),
        ],
        compiler_params=pltpu.CompilerParams(
            collective_id=2, has_side_effects=True, vmem_limit_bytes=VMEM_LIMIT
        ),
        name="mlp_step",
    )(tokens, part, gain, cot_all, mlp_all, cotangent, gate, up, down)


def turn(field, cos, sin):
    return field * cos + pltpu.roll(field, field.shape[-1] // 2, 1) * sin


def tail_kernel(
    nz,
    scale,
    out_part,
    mid_half,
    grad_half,
    gain_part,
    att,
    q_rot,
    kv,
    probs,
    nm_in,
    tok_in,
    gain_in,
    cos_in,
    sin_in,
    qkv_in,
    wo_in,
    give,
    gq,
    go,
    out_tokens,
    grad_tokens,
    small,
    got,
    mid_low,
    gain_got,
    qkv_w,
    out_w,
    full_q,
    full_o,
    ga,
    gs,
    gpre,
    in_part,
    in_got,
    b_x,
    b_out,
    b_in,
    b_acc,
    out_send,
    out_got,
    small_all,
    local_sem,
    b_xrecv,
    b_xsend,
    b_zrecv,
    b_zsend,
    y_recv,
    y_send,
    s_recv,
    s_send,
    *owner_refs,
):
    at = Spot(nz)
    ndp = 4 * nz
    half, wide = mid_half.shape
    seq = 2 * half
    heads, head_dim = full_o.shape[:2]
    rows = head_dim // ndp
    others = [(lax.rem(at.dp + p, ndp), at.t) for p in range(1, ndp)]
    loads = [
        pltpu.make_async_copy(wo_in, out_w, local_sem.at[0]),
        pltpu.make_async_copy(qkv_in, qkv_w, local_sem.at[1]),
    ]
    for load in loads:
        load.start()
    greet(at, others + [at.yn], line=False)
    wires = Wires()
    sum_q = OwnerSum(at, wires, full_q, rows, owner_refs[:7], owner_refs[14:20])
    sum_o = OwnerSum(at, wires, full_o, rows, owner_refs[7:14], owner_refs[20:26])
    out_line = LineSum(at, wires, b_in, b_out, b_zrecv, b_zsend)

    def swap_y(i, src, dst):
        wires.send(src, dst, y_send.at[i], y_recv.at[i], at.yn)

    def out_across(ks):
        for k in ks:
            wires.send(out_part.at[at.near(k), 1 - at.x], b_x.at[k], b_xsend.at[k], b_xrecv.at[k], at.xn)

    def out_along(ks):
        for k in ks:
            wires.landed(b_x.at[k], b_xrecv.at[k], at)
            b_acc[...] = out_part[at.near(k), at.x].astype(F32) + b_x[k].astype(F32)
            if k:
                out_line.push(k, b_acc)

    far, close = list(range(nz - 1, 1, -1)), [1, 0]
    swap_y(0, grad_half, mid_low.at[at.t])
    swap_y(1, gain_part, gain_got)
    out_across(far)
    mid_low[at.t] = grad_half[...]
    wires.landed(mid_low.at[1 - at.t], y_recv.at[0], at)
    swap_y(2, give.at[0], got.at[0])
    loads[0].wait()
    low = mid_low[...].reshape(seq, wide)
    att_grad = dot(low, out_w[...].reshape(heads * head_dim, wide), NT).astype(BF)
    for h in range(heads):
        ga[h] = att_grad[:, h * head_dim : (h + 1) * head_dim]
    tile = 512

    def weight_grad(full, lhs, rhs_of):
        for j in range(wide // tile):
            cols = slice(j * tile, (j + 1) * tile)
            full[:, :, cols] = dot(lhs, rhs_of(cols), TN).reshape(full.shape[0], head_dim, tile)

    weight_grad(full_o, att[...], lambda cols: mid_low[:, :, cols].reshape(seq, tile))
    sum_o.to_core()

    ga_all = ga[...].reshape(heads * seq, head_dim)
    p = probs[...].reshape(heads * seq, seq)
    key, value = kv[0], kv[1]
    grad_value = dot(p.astype(BF), ga_all, TN).astype(BF)
    grad_p = dot(ga_all, value, NT)
    inner = jnp.sum(p * grad_p, axis=-1, keepdims=True)
    gs[...] = (p * (grad_p - inner)).astype(BF)
    sum_o.across()
    cos, sin = cos_in[...], -sin_in[...]
    grad_q = dot(gs[...], key, NN) * scale
    for h in range(heads):
        gpre[:, h * head_dim : (h + 1) * head_dim] = turn(grad_q[h * seq : (h + 1) * seq], cos, sin).astype(BF)
    grad_k = dot(gs[...], q_rot[...].reshape(heads * seq, head_dim), TN) * scale
    gpre[:, heads * head_dim : (heads + 1) * head_dim] = turn(grad_k, cos, sin).astype(BF)
    gpre[:, (heads + 1) * head_dim :] = grad_value
    loads[1].wait()
    pre = gpre[...]
    in_part[...] = dot(pre, qkv_w[...].reshape((heads + 2) * head_dim, wide), NN).astype(BF)
    swap_y(3, in_part, in_got)
    swap_y(4, give.at[1], got.at[1])
    out_along(far)
    weight_grad(full_q, pre, lambda cols: nm_in[:, cols])
    sum_q.to_core()
    bias = jnp.sum(pre.astype(F32), axis=0, keepdims=True)
    sum_q.across()
    out_across(close)
    sum_o.along(go)
    wires.landed(in_got, y_recv.at[3], at)
    grad_in = in_part[...].astype(F32) + in_got[...].astype(F32)
    tok = tok_in[...].astype(F32)
    rms = lax.rsqrt(jnp.mean(tok * tok, axis=-1, keepdims=True) + EPS)
    unit = tok * rms
    grad_gain = jnp.sum(grad_in * unit, axis=0, keepdims=True)
    scaled = grad_in * gain_in[...]
    grad_tokens[...] = mid_low[...].reshape(seq, wide).astype(F32) + rms * (
        scaled - unit * jnp.mean(scaled * unit, axis=-1, keepdims=True)
    )
    wires.landed(gain_got, y_recv.at[1], at)
    gmlp = gain_part[...] + gain_got[...]
    lanes = small.shape[1]
    steps = wide // lanes
    for i in range(steps):
        small_all[at.dp, i : i + 1, :] = grad_gain[:, i * lanes : (i + 1) * lanes]
        small_all[at.dp, steps + i : steps + i + 1, :] = gmlp[:, i * lanes : (i + 1) * lanes]
    for i in range(bias.shape[1] // lanes):
        small_all[at.dp, 2 * steps + i : 2 * steps + i + 1, :] = bias[:, i * lanes : (i + 1) * lanes]
    for n, device in enumerate(others):
        wires.send(small_all.at[at.dp], small_all.at[at.dp], s_send.at[n], s_recv.at[at.dp], device)
    sum_q.along(gq)
    out_along(close)
    sum_o.close(go)
    sum_q.close(gq)
    out_line.close(b_acc)
    out_send[...] = (b_acc[...] + mid_half[...]).astype(BF)
    swap_y(5, out_send, out_got)
    out_tokens[at.t] = out_send[...]
    for device in others:
        wires.landed(small_all.at[device[0]], s_recv.at[device[0]], at)
    total = small_all[0]
    for n in range(1, ndp):
        total = total + small_all[n]
    small[...] = total
    for i in range(2):
        wires.landed(got.at[i], y_recv.at[2 + 2 * i], at)
    wires.landed(out_got, y_recv.at[5], at)
    out_tokens[1 - at.t] = out_got[...]
    wires.drain()


def tail_step(nz, scale, out_part, mid_half, grad_half, gain_part, att, q_rot, kv, probs, nm_in, tokens, gain, cos, sin, qkv, wo, give):
    ndp = 4 * nz
    half, wide = mid_half.shape
    seq = 2 * half
    heads, head_dim = wo.shape[:2]
    rows = head_dim // ndp
    shape = jax.ShapeDtypeStruct
    dma = pltpu.SemaphoreType.DMA
    vm = pltpu.VMEM
    lanes = wide // 3
    srows = 6 + (heads + 2) * head_dim // lanes
    return pl.pallas_call(
        functools.partial(tail_kernel, nz, scale),
        out_shape=(
            shape(((heads + 2) * rows, wide), F32),
            shape((heads * rows, wide), F32),
            shape((2, half, wide), BF),
            shape((seq, wide), F32),
            shape((srows, lanes), F32),
            shape(give.shape, BF),
        ),
        in_specs=[VM] * 13 + [ANY] * 3,
        out_specs=[VM] * 5 + [ANY],
        scratch_shapes=[
            vm((2, half, wide), BF),
            vm((1, wide), F32),
            vm(qkv.shape, BF),
            vm(wo.shape, BF),
            vm((heads + 2, head_dim, wide), F32),
            vm((heads, head_dim, wide), F32),
            vm((heads, seq, head_dim), BF),
            vm((heads * seq, seq), BF),
            vm((seq, (heads + 2) * head_dim), BF),
            vm((seq, wide), BF),
            vm((seq, wide), BF),
            vm((nz, half, wide), BF),
            vm((nz, half, wide), BF),
            vm((2, nz, half, wide), BF),
            vm((half, wide), F32),
            vm((half, wide), BF),
            vm((half, wide), BF),
            vm((ndp, srows, lanes), F32),
            dma((2,)),
            dma((nz,)),
            dma((nz,)),
            dma((2, nz)),
            dma((nz,)),
            dma((6,)),
            dma((6,)),
            dma((ndp,)),
            dma((ndp,)),
        ]
        + OwnerSum.buffers(nz, heads + 2, rows, wide)
        + OwnerSum.buffers(nz, heads, rows, wide)
        + OwnerSum.semaphores(nz)
        + OwnerSum.semaphores(nz),
        compiler_params=pltpu.CompilerParams(
            collective_id=3, has_side_effects=True, vmem_limit_bytes=VMEM_LIMIT
        ),
        name="tail_step",
    )(out_part, mid_half, grad_half, gain_part, att, q_rot, kv, probs, nm_in, tokens, gain, cos, sin, qkv, wo, give)


def rope_tables(seq_len, head_dim):
    half_dim = head_dim // 2
    places = np.arange(seq_len, dtype=np.float32)
    freqs = np.float32(ROPE_BASE) ** (-(np.arange(half_dim, dtype=np.float32) * np.float32(2.0) / np.float32(head_dim)))
    angles = places[:, None] * freqs[None, :]
    cos, sin = np.cos(angles), np.sin(angles)
    return (
        jnp.asarray(np.concatenate([cos, cos], axis=1), F32),
        jnp.asarray(np.concatenate([-sin, sin], axis=1), F32),
    )


def rotate_heads(field, flip_sign):
    half_dim = field.shape[-1] // 2
    places = jnp.arange(field.shape[1], dtype=F32)
    freqs = ROPE_BASE ** (-(jnp.arange(half_dim, dtype=F32) * 2.0 / field.shape[-1]))
    angles = places[:, None] * freqs[None, :]
    cosine = jnp.cos(angles)[None]
    sine = flip_sign * jnp.sin(angles)[None]
    first = field[..., :half_dim]
    second = field[..., half_dim:]
    return jnp.concatenate(
        [first * cosine - second * sine, second * cosine + first * sine], axis=-1
    )


def planes(
    tokens,
    prefix,
    g_attn,
    w_query,
    b_query,
    w_key,
    b_key,
    w_value,
    b_value,
    w_out,
    g_mlp,
    w_gate,
    w_up,
    w_down,
    cotangent,
    ndp,
):
    nz = ndp // 4
    seq_len, wide = tokens.shape
    rows, heads = b_query.shape
    head_dim = rows * ndp
    dp = lax.axis_index("dp")
    gshare = g_attn.shape[0]

    def heads_first(w):
        return jnp.swapaxes(w, 0, 1)

    qkv_own = jnp.concatenate([heads_first(w_query), heads_first(w_key), heads_first(w_value)], axis=0)
    wo_own = heads_first(w_out)

    def row(v):
        flat = v.reshape(1, -1)
        return jnp.pad(flat, ((0, 0), (0, 128 - flat.shape[1])))

    small_own = jnp.concatenate(
        [row(g_attn), row(g_mlp), row(b_query.T), row(b_value)] + [jnp.zeros((4, 128), BF)], axis=0
    )
    qkv_w, out_w, small, cot_all, mlp_all = gather_weights(
        nz, qkv_own, wo_own, small_own, cotangent, w_gate, w_up, w_down
    )
    gain_in = small[:, 0, :gshare].reshape(1, wide).astype(F32)
    gain_mid = small[:, 1, :gshare].reshape(1, wide).astype(F32)
    query_b = small[:, 2, : heads * rows].reshape(ndp, heads, rows).transpose(1, 0, 2).reshape(heads, 1, head_dim)
    value_b = small[:, 3, :rows].reshape(1, 1, head_dim)
    key_b = b_key.T.reshape(1, 1, head_dim)
    bias = jnp.concatenate([query_b, key_b, value_b], axis=0).astype(F32)

    tok_float = tokens.astype(F32)
    normed_in = normed(tok_float, gain_in).astype(BF)
    pre = jnp.einsum("sd,ked->kse", normed_in, qkv_w, preferred_element_type=F32) + bias
    score_scale = head_dim ** (-0.5)
    rot = rotate_heads(pre[: heads + 1], 1.0).astype(BF)
    query_rot, key_rot = rot[:heads], rot[heads]
    value_low = pre[heads + 1].astype(BF)
    row_index = lax.broadcasted_iota(jnp.int32, (seq_len, seq_len), 0)
    col_index = lax.broadcasted_iota(jnp.int32, (seq_len, seq_len), 1)
    allowed = (col_index <= row_index) | (col_index < prefix[0])
    raw_scores = jnp.einsum("gsd,td->gst", query_rot, key_rot, preferred_element_type=F32) * score_scale
    scores = jnp.where(allowed, raw_scores, NEG_BIG)
    row_peak = jnp.max(scores, axis=-1, keepdims=True)
    shifted_exp = jnp.exp(scores - row_peak)
    row_total = jnp.sum(shifted_exp, axis=-1, keepdims=True)
    probs = shifted_exp / row_total
    probs_low = probs.astype(BF)
    attended = jnp.einsum("gst,td->gsd", probs_low, value_low, preferred_element_type=F32)
    attended_low = attended.astype(BF)
    attn_part = jnp.einsum("gse,ged->sd", attended_low, out_w, preferred_element_type=F32)

    out_part, keep_gate, keep_up, keep_down, give, grad_half, mid_half, gain_part = mlp_step(
        nz, tokens, attn_part, gain_mid, cot_all, mlp_all, cotangent, w_gate, w_up, w_down
    )
    att = jnp.swapaxes(attended_low, 0, 1).reshape(seq_len, heads * head_dim)
    cos, sin = rope_tables(seq_len, head_dim)
    gq, go, out_tokens, grad_tokens, sums, got = tail_step(
        nz,
        score_scale,
        out_part,
        mid_half,
        grad_half,
        gain_part,
        att,
        query_rot,
        jnp.stack([key_rot, value_low]),
        probs,
        normed_in,
        tokens,
        gain_in,
        cos,
        sin,
        qkv_w,
        out_w,
        give,
    )
    gq = gq.reshape(heads + 2, rows, wide).transpose(1, 0, 2)
    go = go.reshape(heads, rows, wide).transpose(1, 0, 2)
    gattn_all = sums[:3].reshape(wide)
    gmlp_all = sums[3:6].reshape(wide)
    bias_all = sums[6:].reshape(heads + 2, head_dim).T
    bias_own = lax.dynamic_slice_in_dim(bias_all, dp * rows, rows, axis=0)
    return (
        out_tokens.reshape(seq_len, wide),
        grad_tokens,
        lax.dynamic_slice_in_dim(gattn_all, dp * gshare, gshare),
        gq[:, :heads],
        bias_own[:, :heads],
        gq[:, heads : heads + 1],
        bias_all[:, heads : heads + 1],
        gq[:, heads + 1 :],
        bias_own[:, heads + 1 :],
        go,
        lax.dynamic_slice_in_dim(gmlp_all, dp * gshare, gshare),
        keep_gate + got[0].astype(F32),
        keep_up + got[1].astype(F32),
        keep_down,
    )


def local(*arrays, ndp):
    rows, heads = arrays[4].shape
    shard = arrays[11].shape[0]
    if ndp % 4 == 0 and rows % 8 == 0 and shard % 8 == 0 and heads * rows <= 128:
        return planes(*arrays, ndp=ndp)
    return whole_gather(*arrays)


def solution(mesh):
    in_specs = (
        P("dp", None),
        P("dp"),
        P("dp"),
        P("dp", "tensor", None),
        P("dp", "tensor"),
        P("dp", "tensor", None),
        P(None, "tensor"),
        P("dp", "tensor", None),
        P("dp", "tensor"),
        P("dp", "tensor", None),
        P("dp"),
        P(("dp", "tensor"), None),
        P(("dp", "tensor"), None),
        P(("dp", "tensor"), None),
        P("dp", None),
    )
    out_specs = (
        P("dp", None),
        P("dp", None),
        P("dp"),
        P("dp", "tensor", None),
        P("dp", "tensor"),
        P("dp", "tensor", None),
        P(None, "tensor"),
        P("dp", "tensor", None),
        P("dp", "tensor"),
        P("dp", "tensor", None),
        P("dp"),
        P(("dp", "tensor"), None),
        P(("dp", "tensor"), None),
        P(("dp", "tensor"), None),
    )
    return jax.shard_map(functools.partial(local, ndp=mesh.shape["dp"]), mesh=mesh, in_specs=in_specs, out_specs=out_specs, check_vma=False)
```

profile of v0, /device:TPU:0, one launch (start us, length us, event | category | flops | bytes accessed | tf_op | source)
XLA Modules:
  0.0 286.5 jit_solution(5985172443795393577)
XLA Ops:
  1.3 0.7 pad.15
  2.0 0.7 pad.18
  2.6 0.7 pad.16
  3.3 1.3 fusion.5
  4.6 0.6 add_rsqrt_fusion
  5.1 0.8 copy.38
  6.0 0.6 concatenate.25.small_in
  6.6 0.6 fusion.13
  7.3 1.1 fusion.17
  8.3 1.6 pad_maximum_fusion.1.qkv_in
  10.0 69.5 %gather_weights.1 = (bf16[8,128,1536]{2,1,0:T(8,128)(2,1)}, bf16[6,128,1536]{2,1,0:T(8,128)(2,1)}, bf16[16,8,128]{2,1,0:T(8,128)(2,1)}, bf16[4,2,96,1536]{3,2,1,0:T(8,128)(2,1)}, bf16[3,4,280,1536]{3,2,1,0:T(8,128)(2,1)}) custom-call(bf16[8,8,1536]{2,1,0:T(8,128)(2,1)} %pad_maximum_fusion.1.qkv_in, bf16[6,8,1536]{2,1,0:T(8,128)(2,1)} %bitcast.70, ...), custom_call_target="tpu_custom_call" | custom-call | tf_op jit(solution)/shard_map/gather_weights/pallas_call | solution.py:613
  79.5 0.8 slice_reduce_fusion
  80.3 0.1 concatenate.28
  80.3 0.8 slice.64
  81.2 0.8 slice_convert_fusion.1
  82.0 0.9 convert_reduce_fusion
  82.9 0.7 reshape.198.gain_in
  83.6 0.7 reshape.199.gain_in
  84.4 0.1 concatenate.26
  84.5 0.7 maximum_convert_fusion
  85.2 1.3 fusion.7.nm_in
  86.5 3.3 %fusion.4 = f32[8,192,128]{2,1,0:T(8,128)S(1)} fusion(bf16[8,128,1536]{2,1,0:T(8,128)(2,1)} %get-tuple-element.33.qkv_in, bf16[192,1536]{1,0:T(8,128)(2,1)S(1)} %fusion.7.nm_in, f32[8,128]{1,0:T(8,128)S(1)} %maximum_convert_fusion), kind=kOutput, calls=%fused_computation.11 | convolution fusion | flops 604176384 | bytes 4526080 | tf_op jit(solution)/shard_map/sd,ked->kse/dot_general | solution.py:1243
  89.8 0.3 subtract_convert_fusion
  90.2 0.7 pad_maximum_fusion.2.kv
  90.9 0.9 pad_maximum_fusion.q_rot
  91.8 0.9 fusion.35
  92.7 0.2 broadcast_divide_fusion.probs
  93.0 1.0 copy-done
  94.0 0.3 convolution_convert_fusion
  94.3 0.8 copy_bitcast_fusion.1.att
  95.0 1.6 convolution_bitcast_fusion.part_in
  96.7 93.1 %mlp_step.1 = (bf16[4,2,96,1536]{3,2,1,0:T(8,128)(2,1)}, f32[280,1536]{1,0:T(8,128)}, f32[280,1536]{1,0:T(8,128)}, f32[280,1536]{1,0:T(8,128)}, bf16[2,280,1536]...) custom-call(bf16[192,1536]{1,0:T(8,128)(2,1)} %tok_in.3, ...), custom_call_target="tpu_custom_call" | custom-call | tf_op jit(solution)/shard_map/mlp_step/pallas_call | solution.py:870
  189.8 82.5 %tail_step.1 = (f32[64,1536]{1,0:T(8,128)}, f32[48,1536]{1,0:T(8,128)}, bf16[2,96,1536]{2,1,0:T(8,128)(2,1)}, f32[192,1536]{1,0:T(8,128)}, f32[8,512]{1,0:T(8,128)}, /*index=5*/bf16[2,280,1536]{2,1,0:T(8,128)(2,1)}) custom-call(bf16[4,2,96,1536]{3,2,1,0:T(8,128)(2,1)} %get-tuple-element.38.out_part, f32[96,1536]{1,0:T(8,128)} %get-tuple-element.39.mid_half, ...), custom_call_target="tpu_custom_call" | custom-call | tf_op jit(solution)/shard_map/tail_step/pallas_call | solution.py:1115
  272.3 4.8 %convert_add_fusion = (f32[280,1536]{1,0:T(8,128)}, f32[280,1536]{1,0:T(8,128)}) fusion(f32[280,1536]{1,0:T(8,128)} %get-tuple-element.50, bf16[2,280,1536]{2,1,0:T(8,128)(2,1)} %get-tuple-element.49, f32[280,1536]{1,0:T(8,128)} %get-tuple-element.48), kind=kLoop, calls=%fused_computation.2 | loop fusion | flops 1720320 | bytes 8601600 | tf_op jit(solution)/shard_map/add | solution.py:1306
  277.2 0.6 dynamic_slice.11
  277.8 0.5 slice.77
  278.4 0.5 slice.79
  278.9 0.7 copy.45
  279.6 0.6 dynamic_slice.9
  280.2 0.2 copy.50
  280.4 0.7 fusion.33
  281.1 0.9 copy.44
  282.0 0.8 copy.56
  282.9 1.0 copy.57
  283.9 0.1 copy-done.9
  284.0 0.7 copy.58
  284.7 0.1 copy-done.3
  284.8 1.2 copy.59
  (37 shorter events, 0.6 us)
Async XLA Ops:
  86.4 3.3 %copy-start.2 = (bf16[192,1536]{1,0:T(8,128)(2,1)}, bf16[192,1536]{1,0:T(8,128)(2,1)S(1)}, u32[]{:S(2)}) copy-start(bf16[192,1536]{1,0:T(8,128)(2,1)S(1)} %fusion.7.nm_in) | copy-start | bytes 1769476
  86.4 3.4 %copy-start.6 = (f32[192,64]{1,0:T(8,128)S(1)}, f32[192,64]{1,0:T(8,128)}, u32[]{:S(2)}) copy-start(f32[192,64]{1,0:T(8,128)} %get-tuple-element.90) | copy-start | bytes 147460
  86.5 3.4 %copy-start.7 = (f32[192,64]{1,0:T(8,128)S(1)}, f32[192,64]{1,0:T(8,128)}, u32[]{:S(2)}) copy-start(f32[192,64]{1,0:T(8,128)} %get-tuple-element.91) | copy-start | bytes 147460
  90.1 1.6 copy-start.10
  92.7 2.3 copy-start.1
  93.0 1.0 copy-start
  272.3 4.9 %copy-start.11 = (f32[8,512]{1,0:T(8,128)S(1)}, f32[8,512]{1,0:T(8,128)}, u32[]{:S(2)}) copy-start(f32[8,512]{1,0:T(8,128)} %get-tuple-element.45) | copy-start | bytes 49156
  272.3 7.9 %copy-start.8 = (f32[64,1536]{1,0:T(8,128)S(1)}, f32[64,1536]{1,0:T(8,128)}, u32[]{:S(2)}) copy-start(f32[64,1536]{1,0:T(8,128)} %get-tuple-element.46) | copy-start | bytes 1179652
  277.2 4.9 %copy-start.5 = (bf16[2,96,1536]{2,1,0:T(8,128)(2,1)S(1)}, bf16[2,96,1536]{2,1,0:T(8,128)(2,1)}, u32[]{:S(2)}) copy-start(bf16[2,96,1536]{2,1,0:T(8,128)(2,1)} %get-tuple-element.43) | copy-start | bytes 1769476
  280.4 2.4 copy-start.4
  282.9 1.1 copy-start.9
  282.9 2.0 copy-start.3
where the time goes:
time: 292 us; the launch traced here: 287 us
  Pallas kernels  245 us (84%)
  local copies, waits for them, and re-layouts  17.4 us (6%)
  other arithmetic  15.8 us (5%)
  matrix products  6.17 us (2%)
    pallas_call x1, Pallas kernels, mlp_step(): pl.pallas_call(functools.partial(mlp_kernel, nz), out_shape=(shape((nz, 2...  93.1 us
    pallas_call x1, Pallas kernels, tail_step(): pl.pallas_call(functools.partial(tail_kernel, nz, scale), out_shape=(shap...  82.5 us
    pallas_call x1, Pallas kernels, gather_weights(): pl.pallas_call(functools.partial(gather_kernel, nz), out_shape=(shape((qk...  69.5 us
    unnamed x30, local copies, waits for them, and re-layouts  6.61 us

commit v1 on v0

--- a/solution.py
+++ b/solution.py
@@ -277,6 +277,9 @@
         close = side * half if k % 2 else -side * half
         return z + jnp.where(k <= 2 * edge, close, -side * (k - edge))
 
+    def line(self, k):
+        return (self.index(self.near(k), self.x, self.c), self.t)
+
     def step(self, way):
         z = jnp.clip(self.z + way, 0, self.nz - 1)
         return (self.index(z, self.x, self.c), self.t)
@@ -372,39 +375,20 @@
     def __init__(self, at, wires, inbox, outbox, recv, send):
         self.at, self.wires, self.inbox, self.outbox, self.recv, self.send = at, wires, inbox, outbox, recv, send
 
-    def add(self, way, s, acc_ref, real):
+    def push(self, k, acc_ref):
+        self.outbox[k] = acc_ref[...].astype(BF)
+        self.pass_on(k, self.outbox.at[k])
+
+    def pass_on(self, k, ref):
         at = self.at
-
-        def go():
-            self.wires.landed(self.inbox.at[way, s], self.recv.at[way, s], at)
-            acc_ref[...] += self.inbox[way, s].astype(F32)
-
-        pl.when(real)(go)
-
-    def push(self, k, acc_ref, only=None, again=False):
-        at = self.at
-        s = at.near(k)
-        up = s > at.z
-        way = jnp.where(up, 0, 1)
-        target = at.step(jnp.where(up, 1, -1))
-
-        def fill():
-            self.add(way, s, acc_ref, (up & (at.z > 0)) | ((s < at.z) & (at.z < at.nz - 1)))
-            self.outbox[k] = acc_ref[...].astype(BF)
-
-        fill() if only is None else pl.when(only)(fill)
-        self.wires.send(
-            self.outbox.at[k], self.inbox.at[way, s], self.send.at[k], self.recv.at[way, s], target, only
-        )
-        if only is not None:
-            copy, _ = self.wires.sent.pop()
-            if not again:
-                self.wires.sent.append((copy, None))
+        self.wires.send(ref, self.inbox.at[at.z], self.send.at[k], self.recv.at[at.z], at.line(k))
 
     def close(self, acc_ref):
         at = self.at
-        self.add(0, at.z, acc_ref, at.z > 0)
-        self.add(1, at.z, acc_ref, at.z < at.nz - 1)
+        for k in range(1, at.nz):
+            z = at.near(k)
+            self.wires.landed(self.inbox.at[z], self.recv.at[z], at)
+            acc_ref[...] += self.inbox[z].astype(F32)
 
 
 class OwnerSum:
@@ -425,14 +409,14 @@
             vm((nz,) + block, BF),
             vm((nz,) + block, BF),
             vm((nz,) + block, BF),
-            vm((2, nz) + block, BF),
+            vm((nz,) + block, BF),
             vm(block, F32),
         ]
 
     @staticmethod
     def semaphores(nz):
         dma = pltpu.SemaphoreType.DMA
-        return [dma((nz, 2)), dma((nz, 2)), dma((nz,)), dma((nz,)), dma((2, nz)), dma((nz,))]
+        return [dma((nz, 2)), dma((nz, 2)), dma((nz,)), dma((nz,)), dma((nz,)), dma((nz,))]
 
     def terms(self, z, x, c):
         start = pl.multiple_of(self.at.index(z, x, c) * self.rows, self.rows)
@@ -479,25 +463,25 @@
         self.line.close(out)
 
 
-def greet(at, devices, line=True):
+def greet(devices):
     barrier = pltpu.get_barrier_semaphore()
-
-    def hello(device):
+    for device in devices:
         pl.semaphore_signal(barrier, inc=1, device_id=device, device_id_type=MESH)
-
-    for device in devices:
-        hello(device)
-    count = len(devices)
-    if line:
-        up, down = at.z < at.nz - 1, at.z > 0
-        pl.when(up)(functools.partial(hello, at.step(1)))
-        pl.when(down)(functools.partial(hello, at.step(-1)))
-        count = count + jnp.where(up, 1, 0) + jnp.where(down, 1, 0)
-    pl.semaphore_wait(barrier, count)
-
-
-def gather_kernel(
+    pl.semaphore_wait(barrier, len(devices))
+
+
+def turn(field, cos, sin):
+    return field * cos + pltpu.roll(field, field.shape[-1] // 2, 1) * sin
+
+
+def attn_kernel(
     nz,
+    scale,
+    tok_in,
+    prefix_in,
+    key_b_in,
+    cos_in,
+    sin_in,
     qkv_in,
     wo_in,
     small_in,
@@ -505,14 +489,26 @@
     gate_in,
     up_in,
     down_in,
+    att,
+    q_rot,
+    kv,
+    probs,
+    nm_in,
+    gains,
+    nm_half,
+    mid_half,
     qkv,
     wo,
-    small,
     cot,
     mlp_w,
     stage_a,
     stage_b,
-    stage_c,
+    small,
+    qkv_w,
+    out_w,
+    part,
+    y_out,
+    y_in,
     local_sem,
     q_recv,
     q_send,
@@ -528,16 +524,28 @@
     c_send,
     w_recv,
     w_send,
+    y_recv,
+    y_send,
 ):
     at = Spot(nz)
     ndp = 4 * nz
-    half = cot_in.shape[0] // 2
+    half, wide = mid_half.shape
+    seq = 2 * half
+    units, head_dim = qkv_w.shape[:2]
+    heads = units - 2
     rows = qkv_in.shape[1]
     others = [(lax.rem(at.dp + p, ndp), at.t) for p in range(1, ndp)]
-    greet(at, others + [at.yn], line=False)
+
+    def load(src, dst, i):
+        copy = pltpu.make_async_copy(src, dst, local_sem.at[i])
+        copy.start()
+        return copy
+
+    staged = [load(qkv_in, stage_a, 0), load(wo_in, stage_b, 1), load(small_in, small.at[at.dp], 2)]
+    greet(others + [at.yn])
     wires = Wires()
 
-    def part(ref, core):
+    def part_of(ref, core):
         def slot(z, x):
             owner = at.index(z, x, core)
             return ref.at[:, pl.ds(pl.multiple_of(owner * rows, rows), rows), :]
@@ -547,85 +555,171 @@
     def cot_slot(z, x):
         return cot.at[z, x]
 
-    q_slot, o_slot = part(qkv, at.c), part(wo, at.c)
+    q_slot, o_slot = part_of(qkv, at.c), part_of(wo, at.c)
     gq = Gather(at, wires, q_slot, q_recv, q_send, (q_slot, q_core_recv, q_core_send))
     go = Gather(at, wires, o_slot, o_recv, o_send, (o_slot, o_core_recv, o_core_send))
     gc = Gather(at, wires, cot_slot, c_recv, c_send)
+    mine = at.c * 2 + at.t
+    across = at.c * 2 + 1 - at.t
+
+    def give_weight(i, src):
+        wires.send(src, mlp_w.at[i, mine], w_send.at[0, i], w_recv.at[i, mine], at.yn)
+
+    shard = down_in.shape[0]
+    early = shard * 2 // 7 // 16 * 16
+    pieces = (pl.ds(0, early), pl.ds(early, shard - early))
+
+    def give_down(n):
+        dst = mlp_w.at[2, mine, pieces[n]]
+        wires.send(down_in.at[pieces[n]], dst, w_send.at[0, 2 + n], w_recv.at[2 + n, mine], at.yn)
+
+    for n, device in enumerate(others):
+        wires.send(small_in, small.at[at.dp], s_send.at[n], s_recv.at[at.dp], device)
     gq.start(qkv_in)
+    give_weight(0, gate_in)
+    give_weight(1, up_in)
+    give_down(0)
     go.start(wo_in)
-    mine = at.c * 2 + at.t
     for i, src in enumerate((gate_in, up_in, down_in)):
-        wires.send(src, mlp_w.at[i, mine], w_send.at[0, i], w_recv.at[i, mine], at.yn)
         wires.send(src, mlp_w.at[i, mine], w_send.at[1, i], w_recv.at[i, mine], at.cn)
-    for p, device in enumerate(others):
-        wires.send(small_in, small.at[at.dp], s_send.at[p], s_recv.at[at.dp], device)
-    loads = [
-        pltpu.make_async_copy(qkv_in, stage_a, local_sem.at[0]),
-        pltpu.make_async_copy(wo_in, stage_b, local_sem.at[1]),
-        pltpu.make_async_copy(small_in, stage_c, local_sem.at[2]),
-    ]
-    stores = [
-        pltpu.make_async_copy(stage_a, q_slot(at.z, at.x), local_sem.at[3]),
-        pltpu.make_async_copy(stage_b, o_slot(at.z, at.x), local_sem.at[4]),
-        pltpu.make_async_copy(stage_c, small.at[at.dp], local_sem.at[5]),
-    ]
-    for load in loads:
-        load.start()
-    for load, store in zip(loads, stores):
-        load.wait()
-        store.start()
-    for k in range(1, nz):
+    for copy in staged:
+        copy.wait()
+    placed = [load(stage_a, q_slot(at.z, at.x), 3), load(stage_b, o_slot(at.z, at.x), 4)]
+
+    for device in others:
+        wires.landed(small.at[device[0]], s_recv.at[device[0]], at)
+    lanes = small.shape[2]
+    share = wide // ndp
+    spread = jnp.zeros((small.shape[1], wide), F32)
+    bias = jnp.zeros((8, lanes), F32)
+    blank = jnp.zeros((small.shape[1], wide - lanes), F32)
+    for d in range(ndp):
+        tile = small[d].astype(F32)
+        row = jnp.concatenate([tile, blank], axis=1)
+        spread = spread + (pltpu.roll(row, d * share, 1) if d else row)
+        bias = bias + (pltpu.roll(tile[:8], d * rows, 1) if d else tile[:8])
+    gains[0:1] = spread[0:1]
+    gains[1:2] = spread[8:9]
+
+    gq.relay(1)
+    tok = tok_in[...].astype(F32)
+    rms = lax.rsqrt(jnp.mean(tok * tok, axis=-1, keepdims=True) + EPS)
+    nm_in[...] = (tok * rms * spread[0:1]).astype(BF)
+    go.relay(1)
+    for k in range(2, nz):
         gq.relay(k)
         go.relay(k)
     gc.start(cot_in.at[pl.ds(pl.multiple_of(at.t * half, half), half), :])
     for k in range(nz):
         gq.column(k)
-        go.column(k)
-    for k in range(1, nz):
-        gc.relay(k)
-    for k in range(nz):
-        gc.column(k)
-    across = at.c * 2 + 1 - at.t
-    for i in range(3):
-        wires.landed(mlp_w.at[i, across], w_recv.at[i, across], at)
-        wires.send(mlp_w.at[i, across], mlp_w.at[i, across], w_send.at[2, i], w_recv.at[i, across], at.cn)
-    for i in range(3):
-        for tt in range(2):
-            there = (1 - at.c) * 2 + tt
-            wires.landed(mlp_w.at[i, there], w_recv.at[i, there], at)
-    for device in others:
-        wires.landed(small.at[device[0]], s_recv.at[device[0]], at)
-    for ref, recv in ((qkv, q_core_recv), (wo, o_core_recv)):
-        slot = part(ref, 1 - at.c)
+
+    def core_blocks(ref, recv):
+        slot = part_of(ref, 1 - at.c)
         for z in range(nz):
             for x in range(2):
                 wires.landed(slot(z, x), recv.at[z, x], at)
-    for store in stores:
-        store.wait()
+
+    core_blocks(qkv, q_core_recv)
+    for copy in placed:
+        copy.wait()
+    load(qkv, qkv_w, 5).wait()
+    cos, sin = cos_in[...], sin_in[...]
+    pair = 2 * head_dim
+    for u in range(0, units, 2):
+        pre = dot(nm_in[...], qkv_w[u : u + 2].reshape(pair, wide), NT)
+        for v in range(2):
+            field = pre[:, v * head_dim : (v + 1) * head_dim]
+            if u + v < heads:
+                q_rot[u + v] = turn(field + bias[1 + u + v : 2 + u + v], cos, sin).astype(BF)
+            elif u + v == heads:
+                kv[0] = turn(field + key_b_in[...], cos, sin).astype(BF)
+            else:
+                kv[1] = (field + bias[1 + heads : 2 + heads]).astype(BF)
+    for k in range(nz):
+        go.column(k)
+    scores = (dot(q_rot[...].reshape(heads * seq, head_dim), kv[0], NT) * scale).reshape(heads, seq, seq)
+    row_index = lax.broadcasted_iota(jnp.int32, (seq, seq), 0)
+    col_index = lax.broadcasted_iota(jnp.int32, (seq, seq), 1)
+    allowed = (col_index <= row_index) | (col_index < prefix_in[0])
+    scores = jnp.where(allowed[None], scores, NEG_BIG)
+    shifted = jnp.exp(scores - jnp.max(scores, axis=-1, keepdims=True))
+    probs[...] = shifted / jnp.sum(shifted, axis=-1, keepdims=True)
+    mixed = dot(probs[...].reshape(heads * seq, seq).astype(BF), kv[1], NN).astype(BF)
+    for h in range(heads):
+        att[:, h * head_dim : (h + 1) * head_dim] = mixed[h * seq : (h + 1) * seq]
+    core_blocks(wo, o_core_recv)
+    load(wo, out_w, 6).wait()
+    part[...] = dot(att[...], out_w[...].reshape(heads * head_dim, wide), NN)
+    far_row = pl.multiple_of((1 - at.t) * half, half)
+    own_row = pl.multiple_of(at.t * half, half)
+    y_out[...] = part[pl.ds(far_row, half), :].astype(BF)
+    wires.send(y_out, y_in, y_send.at[0], y_recv.at[0], at.yn)
+    give_down(1)
+    for k in range(1, nz - 1):
+        gc.relay(k)
+    wires.landed(y_in, y_recv.at[0], at)
+    middle = (
+        tok_in[pl.ds(own_row, half), :].astype(F32) + part[pl.ds(own_row, half), :] + y_in[...].astype(F32)
+    )
+    rms = lax.rsqrt(jnp.mean(middle * middle, axis=-1, keepdims=True) + EPS)
+    mid_half[...] = middle
+    nm_half[...] = (middle * rms * gains[1:2]).astype(BF)
+    gc.relay(nz - 1)
+    for k in range(nz):
+        gc.column(k)
+    arrivals = [(mlp_w.at[i, across], i) for i in range(2)]
+    arrivals += [(mlp_w.at[2, across, pieces[n]], 2 + n) for n in range(2)]
+    for ref, i in arrivals:
+        wires.landed(ref, w_recv.at[i, across], at)
+        wires.send(ref, ref, w_send.at[2, i], w_recv.at[i, across], at.cn)
+    there = (1 - at.c) * 2
+    for i in range(3):
+        wires.landed(mlp_w.at[i, there + at.t], w_recv.at[i, there + at.t], at)
+    there = there + 1 - at.t
+    for i in range(2):
+        wires.landed(mlp_w.at[i, there], w_recv.at[i, there], at)
+    for n in range(2):
+        wires.landed(mlp_w.at[2, there, pieces[n]], w_recv.at[2 + n, there], at)
     wires.drain()
 
 
-def gather_weights(nz, qkv, wo, small, cotangent, gate, up, down):
+def attn_step(nz, scale, tokens, prefix, key_b, cos, sin, qkv, wo, small, cotangent, gate, up, down):
     ndp = 4 * nz
-    half, wide = cotangent.shape[0] // 2, cotangent.shape[1]
+    seq, wide = tokens.shape
+    half = seq // 2
+    units, rows = qkv.shape[:2]
+    heads, head_dim = units - 2, ndp * rows
     shape = jax.ShapeDtypeStruct
     dma = pltpu.SemaphoreType.DMA
+    vm = pltpu.VMEM
     return pl.pallas_call(
-        functools.partial(gather_kernel, nz),
+        functools.partial(attn_kernel, nz, scale),
         out_shape=(
-            shape((qkv.shape[0], ndp * qkv.shape[1], wide), BF),
-            shape((wo.shape[0], ndp * wo.shape[1], wide), BF),
-            shape((ndp,) + small.shape, BF),
+            shape((seq, heads * head_dim), BF),
+            shape((heads, seq, head_dim), BF),
+            shape((2, seq, head_dim), BF),
+            shape((heads, seq, seq), F32),
+            shape((seq, wide), BF),
+            shape((2, wide), F32),
+            shape((half, wide), BF),
+            shape((half, wide), F32),
+            shape((units, head_dim, wide), BF),
+            shape((heads, head_dim, wide), BF),
             shape((nz, 2, half, wide), BF),
             shape((3, 4) + gate.shape, BF),
         ),
-        in_specs=[ANY] * 7,
-        out_specs=[ANY] * 5,
+        in_specs=[VM, pl.BlockSpec(memory_space=pltpu.SMEM), VM, VM, VM] + [ANY] * 7,
+        out_specs=[VM] * 8 + [ANY] * 4,
         scratch_shapes=[
-            pltpu.VMEM(qkv.shape, BF),
-            pltpu.VMEM(wo.shape, BF),
-            pltpu.VMEM(small.shape, BF),
-            dma((6,)),
+            vm(qkv.shape, BF),
+            vm(wo.shape, BF),
+            vm((ndp,) + small.shape, BF),
+            vm((units, head_dim, wide), BF),
+            vm((heads, head_dim, wide), BF),
+            vm((seq, wide), F32),
+            vm((half, wide), BF),
+            vm((half, wide), BF),
+            dma((7,)),
             dma((nz, 2)),
             dma((Gather.lanes(nz),)),
             dma((nz, 2)),
@@ -638,34 +732,36 @@
             dma((ndp,)),
             dma((nz, 2)),
             dma((Gather.lanes(nz),)),
+            dma((4, 4)),
             dma((3, 4)),
-            dma((3, 3)),
+            dma((1,)),
+            dma((1,)),
         ],
         compiler_params=pltpu.CompilerParams(
             collective_id=1, has_side_effects=True, vmem_limit_bytes=VMEM_LIMIT
         ),
-        name="gather_weights",
-    )(qkv, wo, small, cotangent, gate, up, down)
+        name="attn_step",
+    )(tokens, prefix, key_b, cos, sin, qkv, wo, small, cotangent, gate, up, down)
 
 
 def mlp_kernel(
     nz,
-    tok_in,
-    part_in,
-    gain_in,
+    nm_in,
+    mid_half,
+    gains,
     cot_in,
     mlp_in,
     cot_own_in,
     gate_in,
     up_in,
     down_in,
-    out_part,
+    out_cols,
+    out_near,
     keep_gate,
     keep_up,
     keep_down,
     give,
     grad_half,
-    mid_half,
     gain_send,
     weights,
     cot,
@@ -681,10 +777,10 @@
     pair,
     grads,
     partner,
-    ysend,
-    yrecv,
     down_send,
     down_recv,
+    o_out,
+    o_in,
     local_sem,
     n_recv,
     n_send,
@@ -694,6 +790,8 @@
     z_send,
     p_recv,
     p_send,
+    o_recv,
+    o_send,
     y_recv,
     y_send,
 ):
@@ -737,40 +835,29 @@
         for s in range(4):
             weights[i, s, shard:padded, :] = jnp.zeros((padded - shard, wide), BF)
 
-    far_row = pl.multiple_of((1 - at.t) * half, half)
-    own_row = pl.multiple_of(at.t * half, half)
-    greet(at, [at.xn, at.yn, at.cn])
-    ysend[...] = part_in[pl.ds(far_row, half), :].astype(BF)
-    wires.send(ysend, yrecv, y_send.at[0], y_recv.at[0], at.yn)
+    loaded_nm = load(nm_in, nm.at[at.z, at.x], local_sem.at[12 + 2 * nz])
+    greet([at.xn, at.yn, at.cn] + [at.line(k) for k in range(1, nz)])
+
+    def nm_slot(z, x):
+        return nm.at[z, x]
+
+    gather = Gather(at, wires, nm_slot, n_recv, n_send)
+    line = LineSum(at, wires, z_in, xr, z_recv, z_send)
+    gather.start(nm_in)
+    gain = gains[1:2]
+    gate_w, up_w, down_w = weights.at[0], weights.at[1], weights.at[2]
     for copy in per[2] + cot_loads:
         copy.wait()
-    down_w = weights.at[2]
-
-    for k in range(nz):
-        zk = at.near(k)
-        gh[zk] = dot(cot[zk].reshape(two, wide), down_w[...].reshape(units, wide), NT)
-
-    wires.landed(yrecv, y_recv.at[0], at)
-    middle = (
-        tok_in[pl.ds(own_row, half), :].astype(F32)
-        + part_in[pl.ds(own_row, half), :]
-        + yrecv[...].astype(F32)
-    )
-    gain = gain_in[...]
-    rms = lax.rsqrt(jnp.mean(middle * middle, axis=-1, keepdims=True) + EPS)
-    mid_half[...] = middle
-    nm[at.z, at.x] = (middle * rms * gain).astype(BF)
-
-    def nm_slot(z, x):
-        return nm.at[z, x]
-
-    gather = Gather(at, wires, nm_slot, n_recv, n_send)
-    line = LineSum(at, wires, z_in, xr, z_recv, z_send)
-    at_end = (at.z == 0) | (at.z == nz - 1)
-    gather.start(nm.at[at.z, at.x])
-    for copy in per[0] + per[1]:
+
+    def hidden_grad(z, carry):
+        gh[z] = dot(cot[z].reshape(two, wide), down_w[...].reshape(units, wide), NT)
+        return carry
+
+    lax.fori_loop(0, nz - 1, hidden_grad, 0)
+    gather.relay(1)
+    hidden_grad(nz - 1, 0)
+    for copy in per[0] + per[1] + [loaded_nm]:
         copy.wait()
-    gate_w, up_w = weights.at[0], weights.at[1]
 
     def hand_over(k):
         wires.send(xs.at[k], xr.at[k], x_send.at[k], x_recv.at[k], at.xn)
@@ -779,10 +866,8 @@
         wires.landed(xr.at[k], x_recv.at[k], at)
         own[k] += xr[k].astype(F32)
         if k:
-            line.push(k, own.at[k], only=at_end)
-
-    if nz > 1:
-        gather.relay(1)
+            line.push(k, own.at[k])
+
     for k in range(nz):
         zk = at.near(k)
         gather.column(k)
@@ -811,12 +896,14 @@
     tile = 512
 
     def weight_grad(i, lhs, rhs):
-        left = lhs[...].reshape(nz * two, units)
-        for j in range(wide // tile):
-            cols = slice(j * tile, (j + 1) * tile)
+        def columns(j, carry):
+            cols = pl.ds(pl.multiple_of(j * tile, tile), tile)
             right = rhs[:, :, :, cols].reshape(nz * two, tile)
-            acc = dot(left, right, TN).astype(BF).reshape(4, padded, tile)
+            acc = dot(lhs[...].reshape(nz * two, units), right, TN).astype(BF).reshape(4, padded, tile)
             grads[i, :, :, cols] = acc[:, :shard]
+            return carry
+
+        lax.fori_loop(0, wide // tile, columns, 0)
         for j in range(2):
             wires.send(
                 grads.at[i, (1 - at.c) * 2 + j], partner.at[i, j], p_send.at[i, j], p_recv.at[i, j], at.cn
@@ -831,14 +918,20 @@
         ).astype(BF)
 
     weight_grad(2, hid, cot)
-    for k in range(nz):
-        zk = at.near(k)
-        out_part[zk] = dot(hid[zk], down_w[...].reshape(units, wide), NN).astype(BF).reshape(2, half, wide)
+    column_sum(nz - 1)
+
+    def mlp_out(z, carry):
+        pair[...] = dot(hid[z], down_w[...].reshape(units, wide), NN).reshape(2, half, wide)
+        o_out[z] = pair[1 - at.x].astype(BF)
+        out_cols[z] = pair[at.x].astype(BF)
+        return carry
+
+    lax.fori_loop(0, nz, mlp_out, 0)
+    for k in range(nz - 1, 0, -1):
+        wires.send(o_out.at[at.near(k)], o_in.at[k], o_send.at[k], o_recv.at[k], at.xn)
+    out_near[...] = o_out[at.z]
     chip_sum(2, keep_down, down_send)
-    wires.send(down_send, down_recv, y_send.at[1], y_recv.at[1], at.yn)
-    column_sum(nz - 1)
-    for k in [nz - 2, nz - 1] + list(range(nz - 3, 0, -1)):
-        line.push(k, own.at[k], only=jnp.logical_not(at_end), again=True)
+    wires.send(down_send, down_recv, y_send.at[0], y_recv.at[0], at.yn)
     weight_grad(0, gg, nm)
     weight_grad(1, gu, nm)
     column_sum(0)
@@ -854,12 +947,16 @@
     grad_half[...] = grad_mid.astype(BF)
     chip_sum(0, keep_gate, give.at[0])
     chip_sum(1, keep_up, give.at[1])
-    wires.landed(down_recv, y_recv.at[1], at)
+    for k in range(nz - 1, 0, -1):
+        wires.landed(o_in.at[k], o_recv.at[k], at)
+        zk = at.near(k)
+        out_cols[zk] = (out_cols[zk].astype(F32) + o_in[k].astype(F32)).astype(BF)
+    wires.landed(down_recv, y_recv.at[0], at)
     keep_down[...] += down_recv[...].astype(F32)
     wires.drain()
 
 
-def mlp_step(nz, tokens, part, gain, cot_all, mlp_all, cotangent, gate, up, down):
+def mlp_step(nz, nm_half, mid_half, gains, cot_all, mlp_all, cotangent, gate, up, down):
     half, wide = cotangent.shape[0] // 2, cotangent.shape[1]
     shard = gate.shape[0]
     padded = -(-shard // 32) * 32
@@ -870,13 +967,13 @@
     return pl.pallas_call(
         functools.partial(mlp_kernel, nz),
         out_shape=(
-            shape((nz, 2, half, wide), BF),
+            shape((nz, half, wide), BF),
+            shape((half, wide), BF),
             shape((shard, wide), F32),
             shape((shard, wide), F32),
             shape((shard, wide), F32),
             shape((2, shard, wide), BF),
             shape((half, wide), BF),
-            shape((half, wide), F32),
             shape((1, wide), F32),
         ),
         in_specs=[VM, VM, VM] + [ANY] * 6,
@@ -892,41 +989,40 @@
             vm((nz, half, wide), F32),
             vm((nz, half, wide), BF),
             vm((nz, half, wide), BF),
-            vm((2, nz, half, wide), BF),
+            vm((nz, half, wide), BF),
             vm((2, half, wide), F32),
             vm((3, 4, shard, wide), BF),
             vm((3, 2, shard, wide), BF),
-            vm((half, wide), BF),
-            vm((half, wide), BF),
             vm((shard, wide), BF),
             vm((shard, wide), BF),
-            dma((12 + 2 * nz + 2,)),
+            vm((nz, half, wide), BF),
+            vm((nz, half, wide), BF),
+            dma((12 + 2 * nz + 1,)),
             dma((nz, 2)),
             dma((Gather.lanes(nz),)),
             dma((nz,)),
             dma((nz,)),
-            dma((2, nz)),
+            dma((nz,)),
             dma((nz,)),
             dma((3, 2)),
             dma((3, 2)),
-            dma((2,)),
-            dma((2,)),
+            dma((nz,)),
+            dma((nz,)),
+            dma((1,)),
+            dma((1,)),
         ],
         compiler_params=pltpu.CompilerParams(
             collective_id=2, has_side_effects=True, vmem_limit_bytes=VMEM_LIMIT
         ),
         name="mlp_step",
-    )(tokens, part, gain, cot_all, mlp_all, cotangent, gate, up, down)
-
-
-def turn(field, cos, sin):
-    return field * cos + pltpu.roll(field, field.shape[-1] // 2, 1) * sin
+    )(nm_half, mid_half, gains, cot_all, mlp_all, cotangent, gate, up, down)
 
 
 def tail_kernel(
     nz,
     scale,
-    out_part,
+    out_cols,
+    out_near,
     mid_half,
     grad_half,
     gain_part,
@@ -960,7 +1056,6 @@
     in_part,
     in_got,
     b_x,
-    b_out,
     b_in,
     b_acc,
     out_send,
@@ -990,30 +1085,20 @@
     ]
     for load in loads:
         load.start()
-    greet(at, others + [at.yn], line=False)
+    greet(others + [at.yn])
     wires = Wires()
     sum_q = OwnerSum(at, wires, full_q, rows, owner_refs[:7], owner_refs[14:20])
     sum_o = OwnerSum(at, wires, full_o, rows, owner_refs[7:14], owner_refs[20:26])
-    out_line = LineSum(at, wires, b_in, b_out, b_zrecv, b_zsend)
+    out_line = LineSum(at, wires, b_in, None, b_zrecv, b_zsend)
 
     def swap_y(i, src, dst):
         wires.send(src, dst, y_send.at[i], y_recv.at[i], at.yn)
 
-    def out_across(ks):
-        for k in ks:
-            wires.send(out_part.at[at.near(k), 1 - at.x], b_x.at[k], b_xsend.at[k], b_xrecv.at[k], at.xn)
-
-    def out_along(ks):
-        for k in ks:
-            wires.landed(b_x.at[k], b_xrecv.at[k], at)
-            b_acc[...] = out_part[at.near(k), at.x].astype(F32) + b_x[k].astype(F32)
-            if k:
-                out_line.push(k, b_acc)
-
-    far, close = list(range(nz - 1, 1, -1)), [1, 0]
     swap_y(0, grad_half, mid_low.at[at.t])
     swap_y(1, gain_part, gain_got)
-    out_across(far)
+    wires.send(out_near, b_x, b_xsend.at[0], b_xrecv.at[0], at.xn)
+    for k in range(nz - 1, 0, -1):
+        out_line.pass_on(k, out_cols.at[at.near(k)])
     mid_low[at.t] = grad_half[...]
     wires.landed(mid_low.at[1 - at.t], y_recv.at[0], at)
     swap_y(2, give.at[0], got.at[0])
@@ -1052,12 +1137,16 @@
     in_part[...] = dot(pre, qkv_w[...].reshape((heads + 2) * head_dim, wide), NN).astype(BF)
     swap_y(3, in_part, in_got)
     swap_y(4, give.at[1], got.at[1])
-    out_along(far)
     weight_grad(full_q, pre, lambda cols: nm_in[:, cols])
     sum_q.to_core()
     bias = jnp.sum(pre.astype(F32), axis=0, keepdims=True)
     sum_q.across()
-    out_across(close)
+    wires.landed(b_x, b_xrecv.at[0], at)
+    b_acc[...] = out_cols[at.z].astype(F32) + b_x[...].astype(F32) + mid_half[...]
+    out_line.close(b_acc)
+    out_send[...] = b_acc[...].astype(BF)
+    swap_y(5, out_send, out_got)
+    out_tokens[at.t] = out_send[...]
     sum_o.along(go)
     wires.landed(in_got, y_recv.at[3], at)
     grad_in = in_part[...].astype(F32) + in_got[...].astype(F32)
@@ -1065,7 +1154,7 @@
     rms = lax.rsqrt(jnp.mean(tok * tok, axis=-1, keepdims=True) + EPS)
     unit = tok * rms
     grad_gain = jnp.sum(grad_in * unit, axis=0, keepdims=True)
-    scaled = grad_in * gain_in[...]
+    scaled = grad_in * gain_in[0:1]
     grad_tokens[...] = mid_low[...].reshape(seq, wide).astype(F32) + rms * (
         scaled - unit * jnp.mean(scaled * unit, axis=-1, keepdims=True)
     )
@@ -1081,13 +1170,8 @@
     for n, device in enumerate(others):
         wires.send(small_all.at[at.dp], small_all.at[at.dp], s_send.at[n], s_recv.at[at.dp], device)
     sum_q.along(gq)
-    out_along(close)
     sum_o.close(go)
     sum_q.close(gq)
-    out_line.close(b_acc)
-    out_send[...] = (b_acc[...] + mid_half[...]).astype(BF)
-    swap_y(5, out_send, out_got)
-    out_tokens[at.t] = out_send[...]
     for device in others:
         wires.landed(small_all.at[device[0]], s_recv.at[device[0]], at)
     total = small_all[0]
@@ -1101,7 +1185,7 @@
     wires.drain()
 
 
-def tail_step(nz, scale, out_part, mid_half, grad_half, gain_part, att, q_rot, kv, probs, nm_in, tokens, gain, cos, sin, qkv, wo, give):
+def tail_step(nz, scale, out_cols, out_near, mid_half, grad_half, gain_part, att, q_rot, kv, probs, nm_in, tokens, gain, cos, sin, qkv, wo, give):
     ndp = 4 * nz
     half, wide = mid_half.shape
     seq = 2 * half
@@ -1122,7 +1206,7 @@
             shape((srows, lanes), F32),
             shape(give.shape, BF),
         ),
-        in_specs=[VM] * 13 + [ANY] * 3,
+        in_specs=[VM] * 14 + [ANY] * 3,
         out_specs=[VM] * 5 + [ANY],
         scratch_shapes=[
             vm((2, half, wide), BF),
@@ -1136,17 +1220,16 @@
             vm((seq, (heads + 2) * head_dim), BF),
             vm((seq, wide), BF),
             vm((seq, wide), BF),
+            vm((half, wide), BF),
             vm((nz, half, wide), BF),
-            vm((nz, half, wide), BF),
-            vm((2, nz, half, wide), BF),
             vm((half, wide), F32),
             vm((half, wide), BF),
             vm((half, wide), BF),
             vm((ndp, srows, lanes), F32),
             dma((2,)),
+            dma((1,)),
+            dma((1,)),
             dma((nz,)),
-            dma((nz,)),
-            dma((2, nz)),
             dma((nz,)),
             dma((6,)),
             dma((6,)),
@@ -1161,7 +1244,7 @@
             collective_id=3, has_side_effects=True, vmem_limit_bytes=VMEM_LIMIT
         ),
         name="tail_step",
-    )(out_part, mid_half, grad_half, gain_part, att, q_rot, kv, probs, nm_in, tokens, gain, cos, sin, qkv, wo, give)
+    )(out_cols, out_near, mid_half, grad_half, gain_part, att, q_rot, kv, probs, nm_in, tokens, gain, cos, sin, qkv, wo, give)
 
 
 def rope_tables(seq_len, head_dim):
@@ -1173,20 +1256,6 @@
     return (
         jnp.asarray(np.concatenate([cos, cos], axis=1), F32),
         jnp.asarray(np.concatenate([-sin, sin], axis=1), F32),
-    )
-
-
-def rotate_heads(field, flip_sign):
-    half_dim = field.shape[-1] // 2
-    places = jnp.arange(field.shape[1], dtype=F32)
-    freqs = ROPE_BASE ** (-(jnp.arange(half_dim, dtype=F32) * 2.0 / field.shape[-1]))
-    angles = places[:, None] * freqs[None, :]
-    cosine = jnp.cos(angles)[None]
-    sine = flip_sign * jnp.sin(angles)[None]
-    first = field[..., :half_dim]
-    second = field[..., half_dim:]
-    return jnp.concatenate(
-        [first * cosine - second * sine, second * cosine + first * sine], axis=-1
     )
 
 
@@ -1225,59 +1294,48 @@
         flat = v.reshape(1, -1)
         return jnp.pad(flat, ((0, 0), (0, 128 - flat.shape[1])))
 
+    def lay(v, count):
+        return jnp.pad(v, ((0, count - v.shape[0]), (0, 128 - v.shape[1])))
+
     small_own = jnp.concatenate(
-        [row(g_attn), row(g_mlp), row(b_query.T), row(b_value)] + [jnp.zeros((4, 128), BF)], axis=0
-    )
-    qkv_w, out_w, small, cot_all, mlp_all = gather_weights(
-        nz, qkv_own, wo_own, small_own, cotangent, w_gate, w_up, w_down
-    )
-    gain_in = small[:, 0, :gshare].reshape(1, wide).astype(F32)
-    gain_mid = small[:, 1, :gshare].reshape(1, wide).astype(F32)
-    query_b = small[:, 2, : heads * rows].reshape(ndp, heads, rows).transpose(1, 0, 2).reshape(heads, 1, head_dim)
-    value_b = small[:, 3, :rows].reshape(1, 1, head_dim)
-    key_b = b_key.T.reshape(1, 1, head_dim)
-    bias = jnp.concatenate([query_b, key_b, value_b], axis=0).astype(F32)
-
-    tok_float = tokens.astype(F32)
-    normed_in = normed(tok_float, gain_in).astype(BF)
-    pre = jnp.einsum("sd,ked->kse", normed_in, qkv_w, preferred_element_type=F32) + bias
+        [row(g_attn), lay(b_query.T, heads), lay(b_value.T, 8 - heads - 1), lay(g_mlp[None], 8)], axis=0
+    )
+    cos, sin = rope_tables(seq_len, head_dim)
     score_scale = head_dim ** (-0.5)
-    rot = rotate_heads(pre[: heads + 1], 1.0).astype(BF)
-    query_rot, key_rot = rot[:heads], rot[heads]
-    value_low = pre[heads + 1].astype(BF)
-    row_index = lax.broadcasted_iota(jnp.int32, (seq_len, seq_len), 0)
-    col_index = lax.broadcasted_iota(jnp.int32, (seq_len, seq_len), 1)
-    allowed = (col_index <= row_index) | (col_index < prefix[0])
-    raw_scores = jnp.einsum("gsd,td->gst", query_rot, key_rot, preferred_element_type=F32) * score_scale
-    scores = jnp.where(allowed, raw_scores, NEG_BIG)
-    row_peak = jnp.max(scores, axis=-1, keepdims=True)
-    shifted_exp = jnp.exp(scores - row_peak)
-    row_total = jnp.sum(shifted_exp, axis=-1, keepdims=True)
-    probs = shifted_exp / row_total
-    probs_low = probs.astype(BF)
-    attended = jnp.einsum("gst,td->gsd", probs_low, value_low, preferred_element_type=F32)
-    attended_low = attended.astype(BF)
-    attn_part = jnp.einsum("gse,ged->sd", attended_low, out_w, preferred_element_type=F32)
-
-    out_part, keep_gate, keep_up, keep_down, give, grad_half, mid_half, gain_part = mlp_step(
-        nz, tokens, attn_part, gain_mid, cot_all, mlp_all, cotangent, w_gate, w_up, w_down
-    )
-    att = jnp.swapaxes(attended_low, 0, 1).reshape(seq_len, heads * head_dim)
-    cos, sin = rope_tables(seq_len, head_dim)
+    att, q_rot, kv, probs, nm_in, gains, nm_half, mid_half, qkv_w, out_w, cot_all, mlp_all = attn_step(
+        nz,
+        score_scale,
+        tokens,
+        prefix,
+        b_key.T.astype(F32),
+        cos,
+        sin,
+        qkv_own,
+        wo_own,
+        small_own,
+        cotangent,
+        w_gate,
+        w_up,
+        w_down,
+    )
+    out_cols, out_near, keep_gate, keep_up, keep_down, give, grad_half, gain_part = mlp_step(
+        nz, nm_half, mid_half, gains, cot_all, mlp_all, cotangent, w_gate, w_up, w_down
+    )
     gq, go, out_tokens, grad_tokens, sums, got = tail_step(
         nz,
         score_scale,
-        out_part,
+        out_cols,
+        out_near,
         mid_half,
         grad_half,
         gain_part,
         att,
-        query_rot,
-        jnp.stack([key_rot, value_low]),
+        q_rot,
+        kv,
         probs,
-        normed_in,
+        nm_in,
         tokens,
-        gain_in,
+        gains,
         cos,
         sin,
         qkv_w,
@@ -1311,7 +1369,7 @@
 def local(*arrays, ndp):
     rows, heads = arrays[4].shape
     shard = arrays[11].shape[0]
-    if ndp % 4 == 0 and rows % 8 == 0 and shard % 8 == 0 and heads * rows <= 128:
+    if ndp % 4 == 0 and rows % 8 == 0 and shard % 8 == 0 and heads <= 6 and arrays[6].shape[1] == 1:
         return planes(*arrays, ndp=ndp)
     return whole_gather(*arrays)
 

time: 292 us -> 252 us (0.86); the launches traced: 287 us -> 251 us
  Pallas kernels: 245 us -> 232 us
  local copies, waits for them, and re-layouts: 17.4 us -> 9.52 us
  other arithmetic: 15.8 us -> 8.94 us
  matrix products: 6.17 us -> 0 us
    pallas_call x1, Pallas kernels: 82.5 us -> 72.8 us  [tail_step(): pl.pallas_call(functools.partial(tail_kernel, nz, scale), out_shape=(shap...]
    dot_general x3 -> x0, matrix products: 5.24 us -> none  [the longest x1 3.3 us: planes(): jnp.einsum('sd,ked->kse', normed_in, qkv_w, preferred_element_type=F32)]
    pallas_call x2, Pallas kernels: 163 us -> 159 us  [the longest x1 81.6 us: mlp_step(): pl.pallas_call(functools.partial(mlp_kernel, nz), out_shape=(shape((nz, h...]
    unnamed x30 -> x19, local copies, waits for them, and re-layouts: 6.61 us -> 6.26 us
where the time goes in v1:
time: 252 us; the launch traced here: 251 us
  Pallas kernels  232 us (92%)
  local copies, waits for them, and re-layouts  9.52 us (4%)
  other arithmetic  8.94 us (4%)
    pallas_call x1, Pallas kernels, mlp_step(): pl.pallas_call(functools.partial(mlp_kernel, nz), out_shape=(shape((nz, h...  81.6 us
    pallas_call x1, Pallas kernels, attn_step(): pl.pallas_call(functools.partial(attn_kernel, nz, scale), out_shape=(shap...  77.1 us
    pallas_call x1, Pallas kernels, tail_step(): pl.pallas_call(functools.partial(tail_kernel, nz, scale), out_shape=(shap...  72.8 us
    unnamed x19, local copies, waits for them, and re-layouts  6.26 us

profile of v1, /device:TPU:0, one launch (start us, length us, event | category | flops | bytes accessed | tf_op | source)
XLA Modules:
  0.0 251.4 jit_solution(5106552956733010737)
XLA Ops:
  0.6 1.6 pad_maximum_fusion.qkv_in
  2.3 0.8 copy.31
  3.1 1.3 fusion.7.small_in
  4.4 1.2 bitcast_convert_fusion.key_b_in
  6.2 77.1 %attn_step.1 = (bf16[192,768]{1,0:T(8,128)(2,1)}, bf16[6,192,128]{2,1,0:T(8,128)(2,1)}, bf16[2,192,128]{2,1,0:T(8,128)(2,1)}, f32[6,192,192]{2,1,0:T(8,128)}, bf...) custom-call(bf16[192,1536]{1,0:T(8,128)(2,1)} %tok_in.3, ...), custom_call_target="tpu_custom_call" | custom-call | tf_op jit(solution)/shard_map/attn_step/pallas_call | solution.py:695
  83.3 81.6 %mlp_step.1 = (bf16[4,96,1536]{2,1,0:T(8,128)(2,1)}, bf16[96,1536]{1,0:T(8,128)(2,1)}, f32[280,1536]{1,0:T(8,128)}, f32[280,1536]{1,0:T(8,128)}, f32[280,1536]{1...) custom-call(bf16[96,1536]{1,0:T(8,128)(2,1)} %get-tuple-element.40.nm_in, ...), custom_call_target="tpu_custom_call" | custom-call | tf_op jit(solution)/shard_map/mlp_step/pallas_call | solution.py:967
  164.9 72.8 %tail_step.1 = (f32[64,1536]{1,0:T(8,128)}, f32[48,1536]{1,0:T(8,128)}, bf16[2,96,1536]{2,1,0:T(8,128)(2,1)}, f32[192,1536]{1,0:T(8,128)}, f32[8,512]{1,0:T(8,128)}, /*index=5*/bf16[2,280,1536]{2,1,0:T(8,128)(2,1)}) custom-call(bf16[4,96,1536]{2,1,0:T(8,128)(2,1)} %get-tuple-element.45.out_cols, bf16[96,1536]{1,0:T(8,128)(2,1)} %get-tuple-element.46.out_near, ...), custom_call_target="tpu_custom_call" | custom-call | tf_op jit(solution)/shard_map/tail_step/pallas_call | solution.py:1199
  237.7 0.0 copy-start.3
  237.8 0.0 copy-start.5
  237.8 4.8 %convert_add_fusion = (f32[280,1536]{1,0:T(8,128)}, f32[280,1536]{1,0:T(8,128)}) fusion(f32[280,1536]{1,0:T(8,128)} %get-tuple-element.64, bf16[2,280,1536]{2,1,0:T(8,128)(2,1)} %get-tuple-element.63, f32[280,1536]{1,0:T(8,128)} %get-tuple-element.62), kind=kLoop, calls=%fused_computation | loop fusion | flops 1720320 | bytes 8601600 | tf_op jit(solution)/shard_map/add | solution.py:1364
  242.6 0.0 copy-start.2
  242.6 0.0 copy-start.1
  242.6 0.0 copy-done.3
  242.6 0.2 copy.36
  242.8 0.9 copy.33
  243.7 0.7 fusion.9
  244.4 0.0 copy-done.5
  244.5 0.6 dynamic_slice.11
  245.1 0.6 dynamic_slice.9
  245.7 0.1 dynamic-slice_bitcast_fusion
  245.8 0.7 copy.34
  246.4 0.5 slice.40
  246.9 0.5 slice.38
  247.5 0.0 copy-done.2
  247.5 0.0 copy-start.4
  247.5 0.8 copy.42
  248.3 0.0 copy-done.1
  248.3 0.0 copy-start
  248.3 1.0 copy.43
  249.3 0.0 copy-done.4
  249.3 0.7 copy.44
  250.0 0.2 copy-done
  250.2 1.2 copy.45
  (5 shorter events, 0.0 us)
Async XLA Ops:
  237.7 4.9 %copy-start.3 = (f32[64,1536]{1,0:T(8,128)S(1)}, f32[64,1536]{1,0:T(8,128)}, u32[]{:S(2)}) copy-start(f32[64,1536]{1,0:T(8,128)} %get-tuple-element.60) | copy-start | bytes 1179652
  237.8 6.7 %copy-start.5 = (f32[8,512]{1,0:T(8,128)S(1)}, f32[8,512]{1,0:T(8,128)}, u32[]{:S(2)}) copy-start(f32[8,512]{1,0:T(8,128)} %get-tuple-element.59) | copy-start | bytes 49156
  242.6 4.9 %copy-start.2 = (bf16[2,96,1536]{2,1,0:T(8,128)(2,1)S(1)}, bf16[2,96,1536]{2,1,0:T(8,128)(2,1)}, u32[]{:S(2)}) copy-start(bf16[2,96,1536]{2,1,0:T(8,128)(2,1)} %get-tuple-element.57) | copy-start | bytes 1769476
  242.6 5.7 %copy-start.1 = (f32[192,1536]{1,0:T(8,128)S(1)}, f32[192,1536]{1,0:T(8,128)}, u32[]{:S(2)}) copy-start(f32[192,1536]{1,0:T(8,128)} %get-tuple-element.101) | copy-start | bytes 3538948
  247.5 1.8 copy-start.4
  248.3 1.9 copy-start
